TPU v7x, 32 devices: a whole 2x2x4 slice. The times are simulated.
32 devices in a mesh: dp: 4 (over y, x), loop: 8 (over z, core).
Axes of the slice: x: 2, y: 2, z: 4, core: 2. Of those that a mesh axis runs over, the one named last changes fastest.
Arguments:
- features: bfloat16 [24, 7, 7, 2048], P('loop'), may hold values from -6 to 6
- image_ids: int32 [24], P('loop'), may hold values from 0 to 15
- text_embeds: bfloat16 [16, 1152], P('loop'), may hold values from -6 to 6
- text_ids: int32 [16], replicated, may hold values from 0 to 15, each once
- depth_kernel: bfloat16 [7, 7, 2048], replicated, may hold values from -0.875 to 0.875
- depth_bias: float32 [2048], replicated, may hold values from -3 to 3
- norm_gain: float32 [2048], replicated, may hold values from 0.5 to 2
- w_up: bfloat16 [2048, 4096], P(None, 'dp'), may hold values from -0.125 to 0.125
- w_down: bfloat16 [2048, 4096], P(None, 'dp'), may hold values from -0.09375 to 0.09375
- projection: bfloat16 [2048, 1152], replicated, may hold values from -0.125 to 0.125
- logit_scale: float32 [1], replicated, may hold values from 4 to 16
- logit_bias: float32 [1], replicated, may hold values from -4 to -1
Outputs:
- row_loss: float32 [24], P('loop')
- grad_texts: float32 [16, 1152], P('loop')
- grad_kernel: float32 [7, 7, 2048], replicated
- grad_bias: float32 [2048], replicated
- grad_gain: float32 [2048], replicated
- grad_up: float32 [2048, 4096], P('loop', 'dp')
- grad_down: float32 [2048, 4096], P('loop', 'dp')
- grad_proj: float32 [2048, 1152], P(('dp', 'loop'))
Inputs may be any that keep to these rules, and one draw needn't show every extreme that they name: `image_ids`: each image's pair id names one text. `text_ids`: the 16 texts carry distinct pair ids.
All inputs are finite; a program needn't handle non-finite values.
Results may differ from a plain program's by a relative error of at most 0.0065.
Values sent between devices are 32-bit elements; how exact they have to be, the bound alone decides.
A program may use at most 192 MiB of HBM per device.

v0:
```python
import jax
import jax.numpy as jnp
import numpy as np
from jax import lax
from jax.sharding import PartitionSpec as P

GRID = 7


full_precision = lax.Precision.HIGHEST
half_root = 0.7071067811865476
density_factor = 0.3989422804014327


def shifted(shard, axis, by):
    count = lax.axis_size(axis)
    return lax.ppermute(shard, axis, [(i, (i + by) % count) for i in range(count)])


def gelu_value(values):
    return 0.5 * values * (1.0 + lax.erf(values * half_root))


def gelu_slope(values):
    cumulative = 0.5 * (1.0 + lax.erf(values * half_root))
    return cumulative + values * jnp.exp(-0.5 * values * values) * density_factor


def depthwise(images, kernel):
    side = kernel.shape[0]
    reach = (side - 1) // 2
    height = images.shape[1]
    width = images.shape[2]
    padded = jnp.pad(images, ((0, 0), (reach, reach), (reach, reach), (0, 0)))
    total = jnp.zeros(images.shape, jnp.float32)
    for row_off in range(side):
        for col_off in range(side):
            window = padded[:, row_off : row_off + height, col_off : col_off + width, :].astype(
                jnp.float32
            )
            total = total + window * kernel[row_off, col_off]
    return total


def kernel_grad(images, grad_conv, side):
    reach = (side - 1) // 2
    height = images.shape[1]
    width = images.shape[2]
    padded = jnp.pad(images, ((0, 0), (reach, reach), (reach, reach), (0, 0)))
    positions = np.arange(width)
    rows_out = []
    for row_off in range(side):
        slab = padded[:, row_off : row_off + height, :, :].astype(jnp.float32)
        cross = jnp.einsum("npsc,npqc->sqc", slab, grad_conv, precision=full_precision)
        cols_out = []
        for col_off in range(side):
            cols_out.append(jnp.sum(cross[positions + col_off, positions], axis=0))
        rows_out.append(jnp.stack(cols_out, axis=0))
    return jnp.stack(rows_out, axis=0)


def norm_parts(images, depth_kernel, depth_bias, norm_gain):
    conv_out = depthwise(images, depth_kernel.astype(jnp.float32)) + depth_bias
    centered = conv_out - jnp.mean(conv_out, axis=3, keepdims=True)
    inv_std = lax.rsqrt(jnp.mean(centered * centered, axis=3, keepdims=True) + 1e-06)
    unit_part = centered * inv_std
    normed = (unit_part * norm_gain).astype(jnp.bfloat16)
    return (unit_part, inv_std, normed)


def unit_rows(values):
    inverse = lax.rsqrt(jnp.sum(values * values, axis=1, keepdims=True) + 1e-06)
    return (values * inverse, inverse)


def conv_grads(images, depth_kernel, unit_part, inv_std, norm_gain, grad_normed):
    grad_gain = jnp.sum(grad_normed * unit_part, axis=(0, 1, 2))
    grad_unit = grad_normed * norm_gain
    grad_conv = inv_std * (
        grad_unit
        - jnp.mean(grad_unit, axis=3, keepdims=True)
        - unit_part * jnp.mean(grad_unit * unit_part, axis=3, keepdims=True)
    )
    grad_bias = jnp.sum(grad_conv, axis=(0, 1, 2))
    grad_kernel = kernel_grad(images, grad_conv, depth_kernel.shape[0])
    return (grad_kernel, grad_bias, grad_gain)


def on_device(
    features,
    image_ids,
    text_embeds,
    text_ids,
    depth_kernel,
    depth_bias,
    norm_gain,
    w_up,
    w_down,
    projection,
    logit_scale,
    logit_bias,
):
    image_rows = features.shape[0]
    channels = features.shape[3]
    hidden_share = w_up.shape[1]
    cell_count = GRID * GRID
    loop_count = lax.axis_size("loop")
    position = lax.axis_index("loop")
    unit_part, inv_std, normed = norm_parts(features, depth_kernel, depth_bias, norm_gain)
    normed_rows = normed.reshape(-1, channels)
    pre_act = jnp.dot(normed_rows, w_up, preferred_element_type=jnp.float32)
    hidden_mean = jnp.mean(
        gelu_value(pre_act).reshape(image_rows, cell_count, hidden_share), axis=1
    ).astype(jnp.bfloat16)
    mlp_part = lax.dot_general(
        hidden_mean, w_down, (((1,), (1,)), ((), ())), preferred_element_type=jnp.float32
    )
    mlp_pool = lax.psum(mlp_part, "dp")
    pooled = (jnp.mean(features.astype(jnp.float32), axis=(1, 2)) + mlp_pool).astype(jnp.bfloat16)
    embedding = jnp.dot(pooled, projection, preferred_element_type=jnp.float32)
    image_unit, image_inverse = unit_rows(embedding)
    text_unit, text_inverse = unit_rows(text_embeds.astype(jnp.float32))
    text_rows = text_embeds.shape[0]
    embed_width = text_embeds.shape[1]
    scale_value = logit_scale[0]
    bias_value = logit_bias[0]

    def pair_tile(block_unit, first_text):
        block_ids = lax.dynamic_slice_in_dim(text_ids, first_text, block_unit.shape[0])
        logits = (
            scale_value * jnp.dot(image_unit, block_unit.T, precision=full_precision) + bias_value
        )
        labels = jnp.where(image_ids[:, None] == block_ids[None, :], 1.0, -1.0).astype(jnp.float32)
        loss_part = -jnp.sum(jax.nn.log_sigmoid(labels * logits), axis=1)
        coeffs = -scale_value * labels * jax.nn.sigmoid(-labels * logits)
        return (loss_part, coeffs)

    def loop_turn(turn_index, carry_state):
        moving, loss_sum, grad_image = carry_state
        block_unit = moving[:text_rows]
        block_grad = moving[text_rows:]
        source = (position - turn_index) % loop_count
        loss_part, coeffs = pair_tile(block_unit, source * text_rows)
        grad_image = grad_image + jnp.dot(coeffs, block_unit, precision=full_precision)
        block_grad = block_grad + jnp.dot(coeffs.T, image_unit, precision=full_precision)
        stacked = jnp.concatenate([block_unit, block_grad], axis=0)
        moving = shifted(stacked, "loop", 1)
        return (moving, loss_sum + loss_part, grad_image)

    start_state = (
        jnp.concatenate([text_unit, jnp.zeros((text_rows, embed_width), jnp.float32)], axis=0),
        jnp.zeros((image_rows,), jnp.float32),
        jnp.zeros((image_rows, embed_width), jnp.float32),
    )
    moving, row_loss, grad_image = lax.fori_loop(0, loop_count, loop_turn, start_state)
    grad_text = moving[text_rows:]
    grad_texts = text_inverse * (
        grad_text - text_unit * jnp.sum(text_unit * grad_text, axis=1, keepdims=True)
    )
    grad_embed = (
        image_inverse
        * (grad_image - image_unit * jnp.sum(image_unit * grad_image, axis=1, keepdims=True))
    ).astype(jnp.bfloat16)
    grad_pooled = lax.dot_general(
        grad_embed, projection, (((1,), (1,)), ((), ())), preferred_element_type=jnp.float32
    ).astype(jnp.bfloat16)
    spread = jnp.dot(grad_pooled, w_down, preferred_element_type=jnp.float32) / cell_count
    grad_pre = (
        (gelu_slope(pre_act).reshape(image_rows, cell_count, hidden_share) * spread[:, None, :])
        .reshape(-1, hidden_share)
        .astype(jnp.bfloat16)
    )
    grad_normed = lax.dot_general(
        grad_pre, w_up, (((1,), (1,)), ((), ())), preferred_element_type=jnp.float32
    ).reshape(features.shape)
    kernel_part, bias_part, gain_part = conv_grads(
        features, depth_kernel, unit_part, inv_std, norm_gain, grad_normed
    )
    grad_kernel, grad_bias, grad_gain = lax.psum(
        (kernel_part, bias_part, gain_part), ("dp", "loop")
    )
    down_term = lax.dot_general(
        grad_pooled, hidden_mean, (((0,), (0,)), ((), ())), preferred_element_type=jnp.float32
    )
    row_share = channels // lax.axis_size("dp")
    pooled_share = lax.dynamic_slice_in_dim(pooled, lax.axis_index("dp") * row_share, row_share, 1)
    proj_term = lax.dot_general(
        pooled_share, grad_embed, (((0,), (0,)), ((), ())), preferred_element_type=jnp.float32
    )
    up_term = lax.dot_general(
        normed_rows, grad_pre, (((0,), (0,)), ((), ())), preferred_element_type=jnp.float32
    )
    grad_up, grad_down, grad_proj = (
        lax.psum_scatter(up_term, "loop", scatter_dimension=0, tiled=True),
        lax.psum_scatter(down_term, "loop", scatter_dimension=0, tiled=True),
        lax.psum_scatter(proj_term, "loop", scatter_dimension=0, tiled=True),
    )
    return (row_loss, grad_texts, grad_kernel, grad_bias, grad_gain, grad_up, grad_down, grad_proj)


def solution(mesh):
    placed = (
        P("loop", None, None, None),
        P("loop"),
        P("loop", None),
        P(),
        P(),
        P(),
        P(),
        P(None, "dp"),
        P(None, "dp"),
        P(),
        P(),
        P(),
    )
    return jax.shard_map(
        on_device,
        mesh=mesh,
        in_specs=placed,
        out_specs=(
            P("loop"),
            P("loop", None),
            P(),
            P(),
            P(),
            P("loop", "dp"),
            P("loop", "dp"),
            P(("dp", "loop"), None),
        ),
        check_vma=False,
    )
```

profile of v0, /device:TPU:0, one launch (start us, length us, event | category | flops | bytes accessed | tf_op | source)
XLA Modules:
  0.0 731.3 jit_solution(5146053782400025438)
XLA Ops:
  9.8 2.0 fusion.63
  11.8 2.1 fusion.62
  13.9 1.9 convert_reduce_fusion
  15.8 4.1 pad_slice_fusion
  20.8 12.0 %fusion.60 = (f32[3,7,7]{2,1,0:T(8,128)S(1)}, f32[3,7,7,2048]{3,2,1,0:T(8,128)S(1)}) fusion(f32[2048]{0:T(1024)} %param.167, f32[2048]{0:T(1024)} %bitcast.201, f32[2048]{0:T(1024)} %bitcast.200, f32[2048]{0:T(1024)} %bitcast.199, f32[2048]{0:T(1024)} %bitcast.198, f32[2048]{0:T(1024)} %bitcast.197, f32[2048]{0:T(1024)} %bitcast.196, ...), kind=kLoop, calls=%fused_computation.218 | loop fusion | flops 44556140 | bytes 2216524 | tf_op jit(solution)/shard_map/reduce_sum | solution.py:64
  35.7 4.3 multiply_multiply_fusion.1
  41.2 3.4 fusion.51
  44.6 18.0 %psum.28 = f32[3,2048]{1,0:T(4,128)S(1)} all-reduce(f32[3,2048]{1,0:T(4,128)S(1)} %fusion.51), channel_id=1, replica_groups=mesh['dp'=4,'loop'=8] {'dp'}, use_global_device_ids=true, to_apply=%region_5.6 | all-reduce | flops 6144 | bytes 49152 | tf_op jit(solution)/shard_map/psum | solution.py:118
  62.7 3.2 multiply_reduce_fusion.5
  66.0 55.6 %while.20 = (s32[]{:T(128)}, f32[4,1152]{1,0:T(4,128)S(1)}, f32[3]{0:T(128)S(1)}, f32[3,1152]{1,0:T(4,128)S(1)}, f32[]{:T(128)}, /*index=5*/s32[3]{0:T(128)S(1)}...) while((s32[]{:T(128)}, f32[4,1152]{1,0:T(4,128)S(1)}, ...), condition=%wide.region_9.10_spmd.clone, body=%wide.region_7.9_spmd.clone.sunk | while | flops 262864 | bytes 270863 | solution.py:155
  68.4 4.6 collective-permute-done
  75.3 4.6 collective-permute-done
  82.3 4.6 collective-permute-done
  89.2 4.6 collective-permute-done
  96.1 4.6 collective-permute-done
  103.1 4.6 collective-permute-done
  110.0 4.6 collective-permute-done
  117.0 4.6 collective-permute-done
  121.8 3.8 convolution_convert_fusion
  129.6 4.9 multiply_reduce_fusion
  134.5 2.3 fusion.59
  136.7 14.9 %copy.168 = f32[3,7,7,2048]{1,2,0,3:T(8,128)} copy(f32[3,7,7,2048]{3,2,1,0:T(8,128)} %get-tuple-element.326) | data formatting | bytes 2408448 | tf_op jit(solution)/shard_map/mul | solution.py:79
  151.7 11.5 %copy.169 = bf16[3,7,13,2048]{2,1,0,3:T(8,128)(2,1)} copy(bf16[3,7,13,2048]{3,2,1,0:T(8,128)(2,1)S(1)} %copy-done.6) | data formatting | bytes 2236416 | tf_op jit(solution)/shard_map/slice | solution.py:53
  163.2 23.4 %convolution_bitcast_fusion.6 = f32[13,7,2048]{0,1,2:T(8,128)} fusion(f32[3,7,7,2048]{1,2,0,3:T(8,128)} %copy.168, bf16[3,7,13,2048]{2,1,0,3:T(8,128)(2,1)} %copy.169), kind=kOutput, calls=%fused_computation.133 | convolution fusion | flops 46964736 | bytes 3067904 | tf_op jit(solution)/shard_map/npsc,npqc->sqc/dot_general | solution.py:54
  186.6 5.3 copy.170
  194.4 13.0 %copy.178 = bf16[3,7,13,2048]{2,1,0,3:T(8,128)(2,1)} copy(bf16[3,7,13,2048]{3,2,1,0:T(8,128)(2,1)} %get-tuple-element.333) | data formatting | bytes 2236416 | tf_op jit(solution)/shard_map/slice | solution.py:53
  207.4 23.5 %convolution_bitcast_fusion.5 = f32[13,7,2048]{0,1,2:T(8,128)} fusion(f32[3,7,7,2048]{1,2,0,3:T(8,128)} %copy.168, bf16[3,7,13,2048]{2,1,0,3:T(8,128)(2,1)} %copy.178), kind=kOutput, calls=%fused_computation.132 | convolution fusion | flops 46964736 | bytes 3067904 | tf_op jit(solution)/shard_map/npsc,npqc->sqc/dot_general | solution.py:54
  230.8 5.3 copy.179
  250.4 13.0 %copy.187 = bf16[3,7,13,2048]{2,1,0,3:T(8,128)(2,1)} copy(bf16[3,7,13,2048]{3,2,1,0:T(8,128)(2,1)} %get-tuple-element.334) | data formatting | bytes 2236416 | tf_op jit(solution)/shard_map/slice | solution.py:53
  263.4 23.7 %convolution_bitcast_fusion.4 = f32[13,7,2048]{0,1,2:T(8,128)} fusion(f32[3,7,7,2048]{1,2,0,3:T(8,128)} %copy.168, bf16[3,7,13,2048]{2,1,0,3:T(8,128)(2,1)} %copy.187), kind=kOutput, calls=%fused_computation.131 | convolution fusion | flops 46964736 | bytes 3067904 | tf_op jit(solution)/shard_map/npsc,npqc->sqc/dot_general | solution.py:54
  287.1 5.3 copy.188
  301.0 13.0 %copy.196 = bf16[3,7,13,2048]{2,1,0,3:T(8,128)(2,1)} copy(bf16[3,7,13,2048]{3,2,1,0:T(8,128)(2,1)} %get-tuple-element.335) | data formatting | bytes 2236416 | tf_op jit(solution)/shard_map/slice | solution.py:53
  314.0 23.3 %convolution_bitcast_fusion.3 = f32[13,7,2048]{0,1,2:T(8,128)} fusion(f32[3,7,7,2048]{1,2,0,3:T(8,128)} %copy.168, bf16[3,7,13,2048]{2,1,0,3:T(8,128)(2,1)} %copy.196), kind=kOutput, calls=%fused_computation.130 | convolution fusion | flops 46964736 | bytes 3067904 | tf_op jit(solution)/shard_map/npsc,npqc->sqc/dot_general | solution.py:54
  337.3 5.3 copy.197
  351.3 11.5 %copy.205 = bf16[3,7,13,2048]{2,1,0,3:T(8,128)(2,1)} copy(bf16[3,7,13,2048]{3,2,1,0:T(8,128)(2,1)S(1)} %get-tuple-element.336) | data formatting | bytes 2236416 | tf_op jit(solution)/shard_map/slice | solution.py:53
  362.8 23.4 %convolution_bitcast_fusion.2 = f32[13,7,2048]{0,1,2:T(8,128)} fusion(f32[3,7,7,2048]{1,2,0,3:T(8,128)} %copy.168, bf16[3,7,13,2048]{2,1,0,3:T(8,128)(2,1)} %copy.205), kind=kOutput, calls=%fused_computation.129 | convolution fusion | flops 46964736 | bytes 3067904 | tf_op jit(solution)/shard_map/npsc,npqc->sqc/dot_general | solution.py:54
  386.2 5.3 copy.206
  396.5 11.5 %copy.214 = bf16[3,7,13,2048]{2,1,0,3:T(8,128)(2,1)} copy(bf16[3,7,13,2048]{3,2,1,0:T(8,128)(2,1)S(1)} %copy-done.5) | data formatting | bytes 2236416 | tf_op jit(solution)/shard_map/slice | solution.py:53
  408.0 23.4 %convolution_bitcast_fusion.1 = f32[13,7,2048]{0,1,2:T(8,128)} fusion(f32[3,7,7,2048]{1,2,0,3:T(8,128)} %copy.168, bf16[3,7,13,2048]{2,1,0,3:T(8,128)(2,1)} %copy.214), kind=kOutput, calls=%fused_computation.128 | convolution fusion | flops 46964736 | bytes 3067904 | tf_op jit(solution)/shard_map/npsc,npqc->sqc/dot_general | solution.py:54
  431.5 5.3 copy.215
  441.8 11.5 %copy.223 = bf16[3,7,13,2048]{2,1,0,3:T(8,128)(2,1)} copy(bf16[3,7,13,2048]{3,2,1,0:T(8,128)(2,1)S(1)} %copy-done.4) | data formatting | bytes 2236416 | tf_op jit(solution)/shard_map/slice | solution.py:53
  453.3 23.5 %convolution_bitcast_fusion = f32[13,7,2048]{0,1,2:T(8,128)} fusion(f32[3,7,7,2048]{1,2,0,3:T(8,128)} %copy.168, bf16[3,7,13,2048]{2,1,0,3:T(8,128)(2,1)} %copy.223), kind=kOutput, calls=%fused_computation.127 | convolution fusion | flops 46964736 | bytes 3067904 | tf_op jit(solution)/shard_map/npsc,npqc->sqc/dot_general | solution.py:54
  476.8 5.3 copy.224
  495.4 2.6 fusion.48
  499.2 4.5 fusion.65
  504.4 4.5 fusion.50
  509.7 37.3 %all-reduce.2 = (f32[2048]{0:T(1024)}, f32[2048]{0:T(1024)}) all-reduce(f32[2048]{0:T(1024)S(1)} %copy-done.67, f32[2048]{0:T(1024)S(1)} %copy-done.66), channel_id=1, replica_groups=mesh['dp'=4,'loop'=8] {'dp','loop'}, use_global_device_ids=true, to_apply=%region_65.66 | all-reduce | flops 4096 | bytes 32768 | tf_op jit(solution)/shard_map/psum | solution.py:179
  547.9 173.6 %all-reduce.5.cloned.1.call-done = f32[7,7,2048]{2,1,0:T(8,128)} async-done(((f32[7,7,2048]{2,1,0:T(8,128)}), f32[7,7,2048]{2,1,0:T(8,128)}) %all-reduce.5.cloned.1.call-update) | async-done | bytes 401424 | tf_op jit(solution)/shard_map/psum | solution.py:179
  (377 shorter events, 90.2 us)
Async XLA Ops:
  8.0 7.8 %copy-start.3 = (bf16[3,7,7,2048]{3,2,1,0:T(8,128)(2,1)S(1)}, bf16[3,7,7,2048]{3,2,1,0:T(8,128)(2,1)}, u32[]{:S(2)}) copy-start(bf16[3,7,7,2048]{3,2,1,0:T(8,128)(2,1)} %param.162) | copy-start | bytes 1806340
  8.0 713.4 %all-reduce.5.cloned.1.call-start = ((), (), s32[]{:S(2)}) async-start(), calls=%async_computation.3 | async-start | bytes 917504 | tf_op jit(solution)/shard_map/psum | solution.py:179
  15.8 4.1 copy-start.64
  20.1 13.1 %copy-start.71 = (f32[2]{0:T(128)}, f32[2]{0:T(128)S(1)}, u32[]{:S(2)}) copy-start(f32[2]{0:T(128)S(1)} %add_rsqrt_fusion.2) | copy-start | bytes 28
  20.8 12.4 %copy-start.57 = (f32[2048]{0:T(1024)S(1)}, f32[2048]{0:T(1024)}, u32[]{:S(2)}) copy-start(f32[2048]{0:T(1024)} %param.168) | copy-start | bytes 24580
  35.7 4.3 copy-start.1
  41.2 21.4 %copy-start.62 = (f32[3,2048]{1,0:T(4,128)S(1)}, f32[3,2048]{1,0:T(4,128)}, u32[]{:S(2)}) copy-start(f32[3,2048]{1,0:T(4,128)} %convert_reduce_fusion) | copy-start | bytes 73732
  65.9 59.7 %copy-start.16 = (f32[3,1152]{1,0:T(4,128)}, f32[3,1152]{1,0:T(4,128)S(1)}, u32[]{:S(2)}) copy-start(f32[3,1152]{1,0:T(4,128)S(1)} %get-tuple-element.390) | copy-start | bytes 41476
  65.9 59.7 %copy-start.68 = (f32[3]{0:T(128)}, f32[3]{0:T(128)S(1)}, u32[]{:S(2)}) copy-start(f32[3]{0:T(128)S(1)} %add_rsqrt_fusion.1) | copy-start | bytes 40
  68.0 5.0 collective-permute-start
  74.9 5.0 collective-permute-start
  81.8 5.0 collective-permute-start
  88.8 5.0 collective-permute-start
  95.7 5.0 collective-permute-start
  102.7 5.0 collective-permute-start
  109.6 5.0 collective-permute-start
  116.5 5.0 collective-permute-start
  121.6 4.1 copy-start.18
  121.6 4.1 copy-start.58
  121.6 4.1 copy-start.70
  121.8 4.5 copy-start
  129.4 5.1 copy-start.7
  136.7 14.9 %copy-start.6 = (bf16[3,7,13,2048]{3,2,1,0:T(8,128)(2,1)S(1)}, bf16[3,7,13,2048]{3,2,1,0:T(8,128)(2,1)}, u32[]{:S(2)}) copy-start(bf16[3,7,13,2048]{3,2,1,0:T(8,128)(2,1)} %get-tuple-element.332) | copy-start | bytes 3354628
  186.6 6.6 copy-start.14
  230.8 7.2 copy-start.13
  236.1 4.4 copy-start.12
  237.4 5.6 copy-start.11
  239.3 6.2 copy-start.10
  241.8 6.2 copy-start.9
  484.6 6.3 copy-start.49
  484.6 6.3 copy-start.48
  485.8 5.1 copy-start.50
  485.8 5.2 copy-start.51
  485.8 5.2 copy-start.52
  485.8 5.3 copy-start.53
  485.8 5.3 copy-start.54
  487.1 4.2 copy-start.24
  487.1 4.3 copy-start.20
  487.1 4.4 copy-start.21
  487.1 4.4 copy-start.22
  487.1 4.5 copy-start.23
  487.1 4.5 copy-start.25
  495.3 226.2 %reduce-scatter.8.cloned.1.call-start = ((), (), s32[]{:S(2)}) async-start(), calls=%async_computation.6 | async-start | bytes 2654208 | tf_op jit(solution)/shard_map/reduce_scatter | solution.py:196
  498.0 223.4 %reduce-scatter.4.cloned.1.call-start = ((), (), s32[]{:S(2)}) async-start(), calls=%async_computation.4 | async-start | bytes 9437184 | tf_op jit(solution)/shard_map/reduce_scatter | solution.py:194
  503.7 217.7 %reduce-scatter.6.cloned.1.call-start = ((), (), s32[]{:S(2)}) async-start(), calls=%async_computation.5 | async-start | bytes 9437184 | tf_op jit(solution)/shard_map/reduce_scatter | solution.py:195
  509.0 38.0 %copy-start.19 = (f32[4,1152]{1,0:T(4,128)S(1)}, f32[4,1152]{1,0:T(4,128)}, u32[]{:S(2)}) copy-start(f32[4,1152]{1,0:T(4,128)} %copy-done.18) | copy-start | bytes 55300
  509.0 38.0 %copy-start.65 = (bf16[2,1152]{1,0:T(2,128)(2,1)S(1)}, bf16[2,1152]{1,0:T(2,128)(2,1)}, u32[]{:S(2)}) copy-start(bf16[2,1152]{1,0:T(2,128)(2,1)} %param.164) | copy-start | bytes 13828
  509.0 38.0 %copy-start.72 = (f32[2]{0:T(128)S(1)}, f32[2]{0:T(128)}, u32[]{:S(2)}) copy-start(f32[2]{0:T(128)} %copy-done.71) | copy-start | bytes 28
  (41 other events, 101.3 us)
Sparse Core Ops, SparseCore 0:
  495.4 225.9 all-reduce.4
Sparse Core Ops, SparseCore 1:
  498.8 33.4 reduce-scatter.7
  535.0 89.0 reduce-scatter.3
  627.0 90.1 reduce-scatter.5
where the time goes:
time: 739 us; the launch traced here: 731 us
  matrix products  213 us (29%)
  waiting for transfers between devices  211 us (29%)
  local copies, waits for them, and re-layouts  210 us (28%)
  blocking collectives  55.4 us (7%)
  other arithmetic  22.8 us (3%)
  between operations  18.2 us (2%)
    psum x1, waiting for transfers between devices, on_device(): lax.psum((kernel_part, bias_part, gain_part), ('dp', 'loop'))  174 us
    dot_general x7, matrix products, kernel_grad(): jnp.einsum('npsc,npqc->sqc', slab, grad_conv, precision=full_precision)  164 us
    slice x8, local copies, waits for them, and re-layouts, kernel_grad(): slab = padded[:, row_off:row_off + height, :, :].astype(jnp.float32)  89 us
    gather x49, local copies, waits for them, and re-layouts, kernel_grad(): cols_out.append(jnp.sum(cross[positions + col_off, positions], axis=0))  52.7 us
    psum x1, blocking collectives, on_device(): lax.psum((kernel_part, bias_part, gain_part), ('dp', 'loop'))  37.3 us
    transpose x7, local copies, waits for them, and re-layouts, kernel_grad(): jnp.einsum('npsc,npqc->sqc', slab, grad_conv, precision=full_precision)  37.1 us
    ppermute x8, waiting for transfers between devices, shifted(): lax.ppermute(shard, axis, [(i, (i + by) % count) for i in range(count)])  36.9 us
    psum x1, blocking collectives, on_device(): mlp_pool = lax.psum(mlp_part, 'dp')  18 us
  transfers between devices with their start and end apart: 12, of which 9 were waited for; matrix products, arithmetic and copies ran while one was open for 2% of the time, Pallas kernels for 0%

commit v1 on v0

v1 whole, which is shorter than its diff:
```python
import functools
import jax
import jax.numpy as jnp
from jax import lax
from jax.experimental import pallas as pl
from jax.experimental.pallas import tpu as pltpu
from jax.sharding import PartitionSpec as P

GRID = 7
LANES = 128
ROWS = 8

full_precision = lax.Precision.HIGHEST
half_root = 0.7071067811865476
density_factor = 0.3989422804014327


def gelu_value(values):
    return 0.5 * values * (1.0 + lax.erf(values * half_root))


def gelu_slope(values):
    cumulative = 0.5 * (1.0 + lax.erf(values * half_root))
    return cumulative + values * jnp.exp(-0.5 * values * values) * density_factor


def unit_rows(values):
    inverse = lax.rsqrt(jnp.sum(values * values, axis=1, keepdims=True) + 1e-06)
    return (values * inverse, inverse)


def lane_tile(index):
    return pl.ds(pl.multiple_of(index * LANES, LANES), LANES)


def shifted_rows(x_ref, lanes, by, cell):
    count = x_ref.shape[0]
    moved = []
    for row in range(GRID):
        per_image = []
        for n in range(count):
            tile = x_ref[n, row, :, lanes]
            if by != 0:
                tile = pltpu.roll(tile, (-by) % ROWS, 0)
            if abs(by) > 1:
                inside = (cell + by >= 0) & (cell + by < GRID)
                tile = jnp.where(inside, tile, 0.0)
            per_image.append(tile)
        moved.append(per_image)
    return moved


def conv_norm_kernel(x_ref, k_ref, bias_ref, unit_ref, inv_ref):
    count = x_ref.shape[0]
    channels = x_ref.shape[3]
    tiles = channels // LANES
    reach = (GRID - 1) // 2
    cell = lax.broadcasted_iota(jnp.int32, (ROWS, LANES), 0)
    cells = [(n, p) for p in range(GRID) for n in range(count)]

    def conv_tile(index, sums):
        lanes = lane_tile(index)
        bias = jnp.broadcast_to(bias_ref[:, lanes], (ROWS, LANES))
        out = {at: bias for at in cells}
        for col_off in range(GRID):
            moved = shifted_rows(x_ref, lanes, col_off - reach, cell)
            for row_off in range(GRID):
                tap = row_off * GRID + col_off
                weight = jnp.broadcast_to(k_ref[tap : tap + 1, lanes], (ROWS, LANES))
                for p in range(GRID):
                    row = p + row_off - reach
                    if 0 <= row < GRID:
                        for n in range(count):
                            out[(n, p)] = out[(n, p)] + moved[row][n] * weight
        for n, p in cells:
            unit_ref[n, p, :, lanes] = out[(n, p)]
        return tuple(total + out[at] for total, at in zip(sums, cells))

    zeros = tuple(jnp.zeros((ROWS, LANES), jnp.float32) for _ in cells)
    sums = lax.fori_loop(0, tiles, conv_tile, zeros)
    means = [jnp.sum(total, axis=1, keepdims=True) / channels for total in sums]
    means = [jnp.broadcast_to(mean, (ROWS, LANES)) for mean in means]

    def square_tile(index, sums):
        lanes = lane_tile(index)
        result = []
        for total, mean, (n, p) in zip(sums, means, cells):
            centered = unit_ref[n, p, :, lanes] - mean
            result.append(total + centered * centered)
        return tuple(result)

    squares = lax.fori_loop(0, tiles, square_tile, zeros)
    inverses = []
    for total, (n, p) in zip(squares, cells):
        variance = jnp.sum(total, axis=1, keepdims=True) / channels
        inverse = jnp.broadcast_to(lax.rsqrt(variance + 1e-06), (ROWS, LANES))
        inverse = jnp.where(cell < GRID, inverse, 0.0)
        inv_ref[n, p, :, :] = inverse
        inverses.append(inverse)

    def norm_tile(index, carry):
        lanes = lane_tile(index)
        for inverse, mean, (n, p) in zip(inverses, means, cells):
            unit = (unit_ref[n, p, :, lanes] - mean) * inverse
            unit_ref[n, p, :, lanes] = unit
        return carry

    lax.fori_loop(0, tiles, norm_tile, 0)


def conv_norm(padded, taps, bias):
    count, _, _, channels = padded.shape
    whole = pl.BlockSpec(memory_space=pltpu.VMEM)
    full = jax.ShapeDtypeStruct(padded.shape, jnp.float32)
    return pl.pallas_call(
        conv_norm_kernel,
        out_shape=(
            full,
            jax.ShapeDtypeStruct((count, GRID, ROWS, LANES), jnp.float32),
        ),
        in_specs=[whole] * 3,
        out_specs=(whole, whole),
        compiler_params=pltpu.CompilerParams(vmem_limit_bytes=24 * 1024 * 1024),
        cost_estimate=pl.CostEstimate(
            flops=2 * 49 * padded.size, bytes_accessed=12 * padded.size, transcendentals=0
        ),
    )(padded, taps, bias)


def conv_grad_kernel(x_ref, unit_ref, inv_ref, gain_ref, grad_ref, out_ref, work_ref):
    count = x_ref.shape[0]
    channels = x_ref.shape[3]
    tiles = channels // LANES
    reach = (GRID - 1) // 2
    taps = GRID * GRID
    cell = lax.broadcasted_iota(jnp.int32, (ROWS, LANES), 0)
    cells = [(n, p) for p in range(GRID) for n in range(count)]
    zero = jnp.zeros((ROWS, LANES), jnp.float32)

    def first_tile(index, carry):
        plain, crossed = carry
        lanes = lane_tile(index)
        gain = jnp.broadcast_to(gain_ref[:, lanes], (ROWS, LANES))
        gain_sum = zero
        plain_out = []
        crossed_out = []
        for at, (n, p) in enumerate(cells):
            unit = unit_ref[n, p, :, lanes]
            grad = grad_ref[n, p, :, lanes]
            gain_sum = gain_sum + grad * unit
            scaled = grad * gain
            plain_out.append(plain[at] + scaled)
            crossed_out.append(crossed[at] + scaled * unit)
        out_ref[taps + 1 : taps + 2, lanes] = jnp.sum(gain_sum, axis=0, keepdims=True)
        return (tuple(plain_out), tuple(crossed_out))

    zeros = tuple(zero for _ in cells)
    plain, crossed = lax.fori_loop(0, tiles, first_tile, (zeros, zeros))
    for at, (n, p) in enumerate(cells):
        first = jnp.sum(plain[at], axis=1, keepdims=True) / channels
        second = jnp.sum(crossed[at], axis=1, keepdims=True) / channels
        work_ref[0, n, p, :, :] = jnp.broadcast_to(first, (ROWS, LANES))
        work_ref[1, n, p, :, :] = jnp.broadcast_to(second, (ROWS, LANES))

    def tap_tile(index, carry):
        lanes = lane_tile(index)
        gain = jnp.broadcast_to(gain_ref[:, lanes], (ROWS, LANES))
        grad_conv = {}
        bias_sum = zero
        for n, p in cells:
            value = inv_ref[n, p, :, :] * (
                grad_ref[n, p, :, lanes] * gain
                - work_ref[0, n, p, :, :]
                - unit_ref[n, p, :, lanes] * work_ref[1, n, p, :, :]
            )
            grad_conv[(n, p)] = value
            bias_sum = bias_sum + value
        out_ref[taps : taps + 1, lanes] = jnp.sum(bias_sum, axis=0, keepdims=True)
        for col_off in range(GRID):
            moved = shifted_rows(x_ref, lanes, col_off - reach, cell)
            for row_off in range(GRID):
                tap = row_off * GRID + col_off
                total = zero
                for p in range(GRID):
                    row = p + row_off - reach
                    if 0 <= row < GRID:
                        for n in range(count):
                            total = total + moved[row][n] * grad_conv[(n, p)]
                out_ref[tap : tap + 1, lanes] = jnp.sum(total, axis=0, keepdims=True)
        return carry

    lax.fori_loop(0, tiles, tap_tile, 0)


def conv_grads(padded, unit, inverse, gain, grad):
    count, _, _, channels = padded.shape
    whole = pl.BlockSpec(memory_space=pltpu.VMEM)
    return pl.pallas_call(
        conv_grad_kernel,
        out_shape=jax.ShapeDtypeStruct((GRID * GRID + 2, channels), jnp.float32),
        in_specs=[whole] * 5,
        out_specs=whole,
        scratch_shapes=[pltpu.VMEM((2, count, GRID, ROWS, LANES), jnp.float32)],
        compiler_params=pltpu.CompilerParams(vmem_limit_bytes=24 * 1024 * 1024),
        cost_estimate=pl.CostEstimate(
            flops=2 * 49 * padded.size, bytes_accessed=12 * padded.size, transcendentals=0
        ),
    )(padded, unit, inverse, gain, grad)


def on_device(
    features,
    image_ids,
    text_embeds,
    text_ids,
    depth_kernel,
    depth_bias,
    norm_gain,
    w_up,
    w_down,
    projection,
    logit_scale,
    logit_bias,
):
    image_rows = features.shape[0]
    channels = features.shape[3]
    hidden_share = w_up.shape[1]
    cell_count = GRID * GRID
    loop_count = lax.axis_size("loop")
    position = lax.axis_index("loop")
    image_count = image_rows * loop_count
    text_rows = text_embeds.shape[0]
    first_image = position * image_rows
    gather = functools.partial(lax.all_gather, axis_name="loop", axis=0, tiled=True)

    text_unit, text_inverse = unit_rows(text_embeds.astype(jnp.float32))
    cell_mean = jnp.mean(features.astype(jnp.float32), axis=(1, 2))
    text_all = gather(text_unit)
    mean_all = gather(cell_mean)
    ids_all = lax.all_gather(image_ids, "loop", axis=0, tiled=True)

    padded = jnp.pad(
        features.astype(jnp.float32), ((0, 0), (0, 0), (0, ROWS - GRID), (0, 0))
    )
    gain_row = norm_gain[None, :]
    unit, inverse = conv_norm(
        padded,
        depth_kernel.astype(jnp.float32).reshape(cell_count, channels),
        depth_bias[None, :],
    )
    padded_rows = image_rows * GRID * ROWS
    unit_rows_own = unit.reshape(padded_rows, channels)
    unit_share = lax.all_to_all(unit_rows_own, "loop", split_axis=1, concat_axis=0, tiled=True)
    normed_rows = (unit_rows_own * gain_row).astype(jnp.bfloat16)
    pre_act = jnp.dot(normed_rows, w_up, preferred_element_type=jnp.float32)
    hidden_sum = jnp.sum(
        gelu_value(pre_act).reshape(image_rows, GRID * ROWS, hidden_share), axis=1
    )
    slope = gelu_slope(pre_act)
    slope_all = gather(slope)
    hidden_all = (gather(hidden_sum) / cell_count).astype(jnp.bfloat16)
    mlp_part = lax.dot_general(
        hidden_all, w_down, (((1,), (1,)), ((), ())), preferred_element_type=jnp.float32
    )
    mlp_pool = lax.psum(mlp_part, "dp")
    pooled = (mean_all + mlp_pool).astype(jnp.bfloat16)
    embedding = jnp.dot(pooled, projection, preferred_element_type=jnp.float32)
    image_unit, image_inverse = unit_rows(embedding)
    logits = (
        logit_scale[0] * jnp.dot(image_unit, text_all.T, precision=full_precision)
        + logit_bias[0]
    )
    labels = jnp.where(ids_all[:, None] == text_ids[None, :], 1.0, -1.0).astype(jnp.float32)
    loss_all = -jnp.sum(jax.nn.log_sigmoid(labels * logits), axis=1)
    row_loss = lax.dynamic_slice_in_dim(loss_all, first_image, image_rows)
    coeffs = -logit_scale[0] * labels * jax.nn.sigmoid(-labels * logits)
    grad_image = jnp.dot(coeffs, text_all, precision=full_precision)
    own_coeffs = lax.dynamic_slice_in_dim(coeffs, position * text_rows, text_rows, 1)
    grad_text = jnp.dot(own_coeffs.T, image_unit, precision=full_precision)
    grad_texts = text_inverse * (
        grad_text - text_unit * jnp.sum(text_unit * grad_text, axis=1, keepdims=True)
    )
    grad_embed = (
        image_inverse
        * (grad_image - image_unit * jnp.sum(image_unit * grad_image, axis=1, keepdims=True))
    ).astype(jnp.bfloat16)
    grad_pooled = lax.dot_general(
        grad_embed, projection, (((1,), (1,)), ((), ())), preferred_element_type=jnp.float32
    ).astype(jnp.bfloat16)
    spread = jnp.dot(grad_pooled, w_down, preferred_element_type=jnp.float32) / cell_count
    own_spread = lax.dynamic_slice_in_dim(spread, first_image, image_rows)
    grad_pre = (
        (slope.reshape(image_rows, GRID * ROWS, hidden_share) * own_spread[:, None, :])
        .reshape(padded_rows, hidden_share)
        .astype(jnp.bfloat16)
    )
    grad_normed = lax.dot_general(
        grad_pre, w_up, (((1,), (1,)), ((), ())), preferred_element_type=jnp.float32
    ).reshape(padded.shape)
    part = conv_grads(padded, unit, inverse, gain_row, grad_normed)
    total = lax.psum(part, ("dp", "loop"))
    grad_kernel = total[:cell_count].reshape(GRID, GRID, channels)
    grad_bias = total[cell_count]
    grad_gain = total[cell_count + 1]

    up_share = channels // loop_count
    grad_pooled_share = lax.dynamic_slice_in_dim(grad_pooled, position * up_share, up_share, 1)
    grad_down = lax.dot_general(
        grad_pooled_share, hidden_all, (((0,), (0,)), ((), ())), preferred_element_type=jnp.float32
    )
    proj_share = up_share // lax.axis_size("dp")
    proj_at = (lax.axis_index("dp") * loop_count + position) * proj_share
    pooled_share = lax.dynamic_slice_in_dim(pooled, proj_at, proj_share, 1)
    grad_proj = lax.dot_general(
        pooled_share, grad_embed, (((0,), (0,)), ((), ())), preferred_element_type=jnp.float32
    )
    grad_pre_all = (
        (slope_all.reshape(image_count, GRID * ROWS, hidden_share) * spread[:, None, :])
        .reshape(loop_count * padded_rows, hidden_share)
        .astype(jnp.bfloat16)
    )
    gain_share = lax.dynamic_slice_in_dim(norm_gain, position * up_share, up_share)
    normed_share = (unit_share * gain_share).astype(jnp.bfloat16)
    grad_up = lax.dot_general(
        normed_share,
        grad_pre_all,
        (((0,), (0,)), ((), ())),
        preferred_element_type=jnp.float32,
    )
    return (row_loss, grad_texts, grad_kernel, grad_bias, grad_gain, grad_up, grad_down, grad_proj)


def solution(mesh):
    placed = (
        P("loop", None, None, None),
        P("loop"),
        P("loop", None),
        P(),
        P(),
        P(),
        P(),
        P(None, "dp"),
        P(None, "dp"),
        P(),
        P(),
        P(),
    )
    return jax.shard_map(
        on_device,
        mesh=mesh,
        in_specs=placed,
        out_specs=(
            P("loop"),
            P("loop", None),
            P(),
            P(),
            P(),
            P("loop", "dp"),
            P("loop", "dp"),
            P(("dp", "loop"), None),
        ),
        check_vma=False,
    )
```

time: 739 us -> 322 us (0.44)
  local copies, waits for them, and re-layouts: 210 us -> 17.3 us
  matrix products: 213 us -> 25.4 us
  waiting for transfers between devices: 211 us -> 181 us
  other arithmetic: 22.8 us -> 10.6 us
  Pallas kernels: 0 us -> 12 us
    dot_general x34 -> x6, matrix products: 193 us -> 10.4 us  [the longest x1 4.1 us: on_device(): lax.dot_general(hidden_all, w_down, (((1,), (1,)), ((), ())), preferred_e...]
    slice x19 -> x1, local copies, waits for them, and re-layouts: 94.9 us -> 1.53 us  [on_device(): grad_gain = total[cell_count + 1]]
    all_gather x0 -> x1, waiting for transfers between devices: none -> 57.8 us  [on_device(): slope_all = gather(slope)]
    psum x2 -> x0, blocking collectives: 55.4 us -> none  [the longest x1 37.3 us: on_device(): lax.psum((kernel_part, bias_part, gain_part), ('dp', 'loop'))]
    gather x49 -> x0, local copies, waits for them, and re-layouts: 52.7 us -> none  [kernel_grad(): cols_out.append(jnp.sum(cross[positions + col_off, positions], axis=0))]
    psum x1 -> x2, waiting for transfers between devices: 174 us -> 122 us  [the longest x1 122 us: on_device(): total = lax.psum(part, ('dp', 'loop'))]
    all_gather x0 -> x3, blocking collectives: none -> 46.2 us  [the longest x1 15.7 us: on_device(): hidden_all = (gather(hidden_sum) / cell_count).astype(jnp.bfloat16)]
    transpose x7 -> x0, local copies, waits for them, and re-layouts: 37.1 us -> none  [kernel_grad(): jnp.einsum('npsc,npqc->sqc', slab, grad_conv, precision=full_precision)]
  transfers between devices with their start and end apart: 12 -> 4, of which waited for: 9 -> 2; matrix products, arithmetic and copies ran while one was open for 2% -> 6% of each run, Pallas kernels for 0% -> 0%
where the time goes in v1:
time: 322 us; the launch traced here: 321 us
  waiting for transfers between devices  181 us (56%)
  blocking collectives  55.7 us (17%)
  matrix products  25.4 us (8%)
  local copies, waits for them, and re-layouts  17.3 us (5%)
  between operations  16 us (5%)
  Pallas kernels  12 us (4%)
  other arithmetic  10.6 us (3%)
  starting transfers between devices  3.82 us (1%)
    psum x1, waiting for transfers between devices, on_device(): total = lax.psum(part, ('dp', 'loop'))  122 us
    all_gather x1, waiting for transfers between devices, on_device(): slope_all = gather(slope)  57.8 us
    all_gather x1, blocking collectives, on_device(): hidden_all = (gather(hidden_sum) / cell_count).astype(jnp.bfloat16)  15.7 us
    all_gather x1, blocking collectives, on_device(): mean_all = gather(cell_mean)  15.5 us
    all_gather x1, blocking collectives, on_device(): text_all = gather(text_unit)  15.1 us
    unnamed x1, blocking collectives  9.46 us
    unnamed x44, local copies, waits for them, and re-layouts  7.99 us
    pallas_call x1, Pallas kernels, conv_grads(): pl.pallas_call(conv_grad_kernel, out_shape=jax.ShapeDtypeStruct((GRID * G...  6.55 us
  transfers between devices with their start and end apart: 4, of which 2 were waited for; matrix products, arithmetic and copies ran while one was open for 6% of the time, Pallas kernels for 0%

profile of v1, /device:TPU:0, one launch (start us, length us, event | category | flops | bytes accessed | tf_op | source)
XLA Modules:
  0.0 321.4 jit_solution(13934168730919445811)
XLA Ops:
  7.2 1.0 reshape.68.k_ref
  8.2 1.2 pad.4.x_ref
  9.5 0.7 copy-done.1
  10.2 5.4 %shard_map.179 = (f32[3,7,8,2048]{3,2,1,0:T(8,128)S(1)}, f32[3,7,8,128]{3,2,1,0:T(8,128)S(1)}) custom-call(f32[3,7,8,2048]{3,2,1,0:T(8,128)S(1)} %pad.4.x_ref, f32[49,2048]{1,0:T(8,128)S(1)} %reshape.68.k_ref, f32[1,2048]{1,0:T(1,128)S(1)} %bitcast.65), custom_call_target="tpu_custom_call" | custom-call | flops 33718272 | bytes 4128768 | tf_op jit(solution)/shard_map/pallas_call | solution.py:115
  15.6 0.1 fusion.4
  15.7 4.0 %multiply_multiply_fusion.1 = (f32[168,1024]{1,0:T(8,128)}, f32[168,1024]{1,0:T(8,128)S(1)}) fusion(bf16[168,2048]{1,0:T(8,128)(2,1)S(1)} %fusion.4, bf16[2048,1024]{1,0:T(8,128)(2,1)} %param.19), kind=kOutput, calls=%fused_computation.20 | convolution fusion | flops 705331200 | bytes 6258688 | tf_op jit(solution)/shard_map/dot_general | solution.py:255
  19.7 1.2 reduce_sum.64
  20.9 15.7 %all-gather.1 = f32[8,3,1024]{2,1,0:T(4,128)S(1)} all-gather(f32[1,3,1024]{2,1,0:T(4,128)S(1)} %bitcast.70), channel_id=1, replica_groups=mesh['dp'=4,'loop'=8] {'loop'}, dimensions={0}, use_global_device_ids=true | all-gather | bytes 110592 | tf_op jit(solution)/shard_map/all_gather | solution.py:261
  36.6 0.7 multiply_convert_fusion
  37.3 1.5 reshape.82
  38.8 4.1 %fusion.41 = f32[24,2048]{1,0:T(8,128)} fusion(bf16[24,1024]{1,0:T(8,128)(2,1)} %reshape.82, bf16[2048,1024]{1,0:T(8,128)(2,1)} %param.20), kind=kOutput, calls=%fused_computation.66 | convolution fusion | flops 100663296 | bytes 4440064 | tf_op jit(solution)/shard_map/dot_general | solution.py:262
  43.0 1.3 convert_reduce_fusion
  44.2 0.1 fusion.24
  44.4 0.6 multiply_bitcast_fusion
  46.4 15.1 %all-gather.2 = f32[8,2,1152]{2,1,0:T(2,128)} all-gather(f32[1,2,1152]{2,1,0:T(2,128)S(1)} %fusion.20), channel_id=1, replica_groups=mesh['dp'=4,'loop'=8] {'loop'}, dimensions={0}, use_global_device_ids=true | all-gather | bytes 82944 | tf_op jit(solution)/shard_map/all_gather | solution.py:238
  61.5 1.6 reshape.77
  63.0 15.5 %all-gather = f32[8,3,2048]{2,1,0:T(4,128)} all-gather(f32[1,3,2048]{2,1,0:T(4,128)} %multiply_bitcast_fusion), channel_id=1, replica_groups=mesh['dp'=4,'loop'=8] {'loop'}, dimensions={0}, use_global_device_ids=true | all-gather | bytes 221184 | tf_op jit(solution)/shard_map/all_gather | solution.py:239
  78.5 1.7 reshape.73
  80.2 1.2 dynamic-slice
  82.1 0.9 dynamic-update-slice
  83.0 9.5 %all-reduce.1 = s32[24]{0:T(128)} all-reduce(s32[24]{0:T(128)S(1)} %dynamic-update-slice), channel_id=1, replica_groups=mesh['dp'=4,'loop'=8] {'loop'}, use_global_device_ids=true, to_apply=%add.1 | all-reduce | flops 24 | bytes 192
  92.4 1.1 add_convert_fusion
  93.5 3.3 %multiply_reduce_fusion.1 = (f32[24]{0:T(128)S(1)}, f32[24,1152]{1,0:T(8,128)S(1)}) fusion(bf16[24,2048]{1,0:T(8,128)(2,1)S(1)} %add_convert_fusion, bf16[2048,1152]{1,0:T(8,128)(2,1)} %param.21), kind=kOutput, calls=%fused_computation.26 | convolution fusion | flops 113301480 | bytes 4927584 | tf_op jit(solution)/shard_map/dot_general | solution.py:267
  96.9 1.5 fusion.26
  98.4 0.4 multiply_reduce_fusion
  99.0 0.6 copy-done.7
  99.6 3.8 %convolution_convert_fusion = bf16[24,2048]{1,0:T(8,128)(2,1)S(1)} fusion(bf16[24,1152]{1,0:T(8,128)(2,1)S(1)} %multiply_convert_fusion.1, bf16[2048,1152]{1,0:T(8,128)(2,1)} %param.21), kind=kOutput, calls=%fused_computation.4 | convolution fusion | flops 113295360 | bytes 4872192 | tf_op jit(solution)/shard_map/dot_general | solution.py:287
  103.4 0.7 convolution_multiply_fusion
  104.1 1.1 fusion.10
  105.3 0.7 copy-done.3
  105.9 1.6 fusion.1.grad_ref
  107.5 6.5 %shard_map.180 = f32[51,2048]{1,0:T(8,128)} custom-call(f32[3,7,8,2048]{3,2,1,0:T(8,128)S(1)} %pad.4.x_ref, f32[3,7,8,2048]{3,2,1,0:T(8,128)S(1)} %get-tuple-element.10.unit_ref, f32[3,7,8,128]{3,2,1,0:T(8,128)S(1)} %get-tuple-element.11.inv_ref, f32[1,2048]{1,0:T(1,128)S(1)} %bitcast.64, f32[3,7,8,2048]{3,2,1,0:T(8,128)S(1)} %fusion.1.grad_ref), custom_call_target="tpu_custom_call" | custom-call | flops 33718272 | bytes 4128768 | tf_op jit(solution)/shard_map/pallas_call | solution.py:198
  114.1 0.7 all-gather.5.cloned.1.call-update
  114.9 0.5 copy.23
  115.4 1.5 copy.21
  116.9 3.7 %all-to-all-start = ((f32[168,8,256]{2,0,1:T(8,128)}), f32[168,8,256]{2,0,1:T(8,128)S(1)}, u32[]{:S(2)}, u32[]{:S(2)}) async-start(f32[168,8,256]{2,0,1:T(8,128)} %copy.21), calls=%async_computation | async-start | bytes 2752512 | tf_op jit(solution)/shard_map/all_to_all | solution.py:253
  120.7 0.6 dynamic_slice.18
  121.3 0.4 fusion.21
  121.7 1.7 fusion.33
  123.4 2.0 fusion.16
  125.4 0.7 fusion.23
  126.1 122.1 %all-reduce.7.cloned.1.call-done = f32[51,2048]{1,0:T(8,128)} async-done(((f32[51,2048]{1,0:T(8,128)}), f32[51,2048]{1,0:T(8,128)}) %all-reduce.7.cloned.1.call-update) | async-done | bytes 417808 | tf_op jit(solution)/shard_map/psum | solution.py:301
  248.1 1.8 reshape.66
  250.0 1.5 fusion.40
  251.5 0.1 fusion.3
  251.6 57.8 %all-gather.5.cloned.1.call-done = f32[1344,1024]{1,0:T(8,128)} async-done(((f32[168,1024]{1,0:T(8,128)}), f32[1344,1024]{1,0:T(8,128)}) %all-gather.5.cloned.1.call-update) | async-done | bytes 5505040 | tf_op jit(solution)/shard_map/all_gather | solution.py:260
  309.5 3.4 %fusion = bf16[1344,1024]{1,0:T(8,128)(2,1)S(1)} fusion(f32[1344,1024]{1,0:T(8,128)} %all-gather.5.cloned.1.call-done, f32[24,1024]{1,0:T(8,128)S(1)} %copy-done.10), kind=kLoop, calls=%fused_computation.1 | loop fusion | flops 2752512 | bytes 8355840 | tf_op jit(solution)/shard_map/convert_element_type | solution.py:320
  312.9 2.0 fusion.42
  (49 shorter events, 0.5 us)
Async XLA Ops:
  7.2 8.4 %copy-start = (f32[2048]{0:T(1024)S(1)}, f32[2048]{0:T(1024)}, u32[]{:S(2)}) copy-start(f32[2048]{0:T(1024)} %param.18) | copy-start | bytes 24580
  7.2 85.3 %all-reduce.5.cloned.1.call-start = ((), (), s32[]{:S(2)}) async-start(), calls=%async_computation.1 | async-start | bytes 393216 | tf_op jit(solution)/shard_map/psum | solution.py:265
  9.5 0.7 copy-start.1
  36.6 7.6 %copy-start.14 = (bf16[2,1152]{1,0:T(2,128)(2,1)S(1)}, bf16[2,1152]{1,0:T(2,128)(2,1)}, u32[]{:S(2)}) copy-start(bf16[2,1152]{1,0:T(2,128)(2,1)} %param.14) | copy-start | bytes 13828
  42.9 205.2 %all-reduce.7.cloned.1.call-start = ((), (), s32[]{:S(2)}) async-start(), calls=%async_computation.2 | async-start | bytes 917504 | tf_op jit(solution)/shard_map/psum | solution.py:301
  44.4 0.6 copy-start.15
  92.4 4.5 %copy-start.6 = (f32[16,1152]{1,0:T(8,128)S(1)}, f32[16,1152]{1,0:T(8,128)}, u32[]{:S(2)}) copy-start(f32[16,1152]{1,0:T(8,128)} %reshape.77) | copy-start | bytes 221188
  92.4 4.5 %copy-start.18 = (s32[24]{0:T(128)S(1)}, s32[24]{0:T(128)}, u32[]{:S(2)}) copy-start(s32[24]{0:T(128)} %all-reduce.1) | copy-start | bytes 292
  93.5 5.3 %copy-start.13 = (bf16[24,2048]{1,0:T(8,128)(2,1)}, bf16[24,2048]{1,0:T(8,128)(2,1)S(1)}, u32[]{:S(2)}) copy-start(bf16[24,2048]{1,0:T(8,128)(2,1)S(1)} %add_convert_fusion) | copy-start | bytes 294916
  93.5 9.9 %copy-start.2 = (bf16[2048,1024]{1,0:T(8,128)(2,1)S(1)}, bf16[2048,1024]{1,0:T(8,128)(2,1)}, u32[]{:S(2)}) copy-start(bf16[2048,1024]{1,0:T(8,128)(2,1)} %param.20) | copy-start | bytes 12582916
  96.9 2.0 copy-start.4
  99.0 0.6 copy-start.7
  103.4 4.1 %copy-start.11 = (bf16[24,2048]{1,0:T(8,128)(2,1)}, bf16[24,2048]{1,0:T(8,128)(2,1)S(1)}, u32[]{:S(2)}) copy-start(bf16[24,2048]{1,0:T(8,128)(2,1)S(1)} %convolution_convert_fusion) | copy-start | bytes 294916
  103.4 2.5 copy-start.3
  104.1 1.2 copy-start.9
  114.1 195.4 %all-gather.5.cloned.1.call-start = ((), (), s32[]{:S(2)}) async-start(), calls=%async_computation.3 | async-start | bytes 6193152 | tf_op jit(solution)/shard_map/all_gather | solution.py:260
  114.8 5.9 %copy-start.17 = (f32[24]{0:T(128)S(1)}, f32[24]{0:T(128)}, u32[]{:S(2)}) copy-start(f32[24]{0:T(128)} %get-tuple-element.17) | copy-start | bytes 292
  114.8 6.5 %copy-start.5 = (f32[24,1152]{1,0:T(8,128)S(1)}, f32[24,1152]{1,0:T(8,128)}, u32[]{:S(2)}) copy-start(f32[24,1152]{1,0:T(8,128)} %copy-done.4) | copy-start | bytes 331780
  114.8 6.5 %copy-start.16 = (f32[2]{0:T(128)S(1)}, f32[2]{0:T(128)}, u32[]{:S(2)}) copy-start(f32[2]{0:T(128)} %copy-done.15) | copy-start | bytes 28
  114.8 6.8 %copy-start.8 = (bf16[24,1152]{1,0:T(8,128)(2,1)S(1)}, bf16[24,1152]{1,0:T(8,128)(2,1)}, u32[]{:S(2)}) copy-start(bf16[24,1152]{1,0:T(8,128)(2,1)} %copy-done.7) | copy-start | bytes 165892
  114.9 8.5 %copy-start.12 = (bf16[24,1024]{1,0:T(8,128)(2,1)S(1)}, bf16[24,1024]{1,0:T(8,128)(2,1)}, u32[]{:S(2)}) copy-start(bf16[24,1024]{1,0:T(8,128)(2,1)} %reshape.82) | copy-start | bytes 147460
  116.9 192.6 %copy-start.10 = (f32[24,1024]{1,0:T(8,128)S(1)}, f32[24,1024]{1,0:T(8,128)}, u32[]{:S(2)}) copy-start(f32[24,1024]{1,0:T(8,128)} %copy-done.9) | copy-start | bytes 294916
  116.9 134.6 %all-to-all-start = ((f32[168,8,256]{2,0,1:T(8,128)}), f32[168,8,256]{2,0,1:T(8,128)S(1)}, u32[]{:S(2)}, u32[]{:S(2)}) async-start(f32[168,8,256]{2,0,1:T(8,128)} %copy.21), calls=%async_computation | async-start | bytes 2752512 | tf_op jit(solution)/shard_map/all_to_all | solution.py:253
Sparse Core Ops, SparseCore 0:
  43.0 43.4 all-reduce.4
  114.2 133.9 all-reduce.6
  250.4 59.0 all-gather.4

commit v2 on v1

--- a/solution.py
+++ b/solution.py
@@ -9,6 +9,7 @@
 GRID = 7
 LANES = 128
 ROWS = 8
+TAP_ROWS = 64
 
 full_precision = lax.Precision.HIGHEST
 half_root = 0.7071067811865476
@@ -121,9 +122,6 @@
         in_specs=[whole] * 3,
         out_specs=(whole, whole),
         compiler_params=pltpu.CompilerParams(vmem_limit_bytes=24 * 1024 * 1024),
-        cost_estimate=pl.CostEstimate(
-            flops=2 * 49 * padded.size, bytes_accessed=12 * padded.size, transcendentals=0
-        ),
     )(padded, taps, bias)
 
 
@@ -142,6 +140,7 @@
         lanes = lane_tile(index)
         gain = jnp.broadcast_to(gain_ref[:, lanes], (ROWS, LANES))
         gain_sum = zero
+        out_ref[index, 48:TAP_ROWS, :] = jnp.zeros((TAP_ROWS - 48, LANES), jnp.float32)
         plain_out = []
         crossed_out = []
         for at, (n, p) in enumerate(cells):
@@ -151,7 +150,7 @@
             scaled = grad * gain
             plain_out.append(plain[at] + scaled)
             crossed_out.append(crossed[at] + scaled * unit)
-        out_ref[taps + 1 : taps + 2, lanes] = jnp.sum(gain_sum, axis=0, keepdims=True)
+        out_ref[index, taps + 1 : taps + 2, :] = jnp.sum(gain_sum, axis=0, keepdims=True)
         return (tuple(plain_out), tuple(crossed_out))
 
     zeros = tuple(zero for _ in cells)
@@ -175,7 +174,7 @@
             )
             grad_conv[(n, p)] = value
             bias_sum = bias_sum + value
-        out_ref[taps : taps + 1, lanes] = jnp.sum(bias_sum, axis=0, keepdims=True)
+        out_ref[index, taps : taps + 1, :] = jnp.sum(bias_sum, axis=0, keepdims=True)
         for col_off in range(GRID):
             moved = shifted_rows(x_ref, lanes, col_off - reach, cell)
             for row_off in range(GRID):
@@ -186,7 +185,7 @@
                     if 0 <= row < GRID:
                         for n in range(count):
                             total = total + moved[row][n] * grad_conv[(n, p)]
-                out_ref[tap : tap + 1, lanes] = jnp.sum(total, axis=0, keepdims=True)
+                out_ref[index, tap : tap + 1, :] = jnp.sum(total, axis=0, keepdims=True)
         return carry
 
     lax.fori_loop(0, tiles, tap_tile, 0)
@@ -197,15 +196,159 @@
     whole = pl.BlockSpec(memory_space=pltpu.VMEM)
     return pl.pallas_call(
         conv_grad_kernel,
-        out_shape=jax.ShapeDtypeStruct((GRID * GRID + 2, channels), jnp.float32),
+        out_shape=jax.ShapeDtypeStruct((channels // LANES, TAP_ROWS, LANES), jnp.float32),
         in_specs=[whole] * 5,
         out_specs=whole,
         scratch_shapes=[pltpu.VMEM((2, count, GRID, ROWS, LANES), jnp.float32)],
         compiler_params=pltpu.CompilerParams(vmem_limit_bytes=24 * 1024 * 1024),
-        cost_estimate=pl.CostEstimate(
-            flops=2 * 49 * padded.size, bytes_accessed=12 * padded.size, transcendentals=0
+    )(padded, unit, inverse, gain, grad)
+
+
+def peer_copies(axis, count, source_of, target, send_sems, recv_sems):
+    me = lax.axis_index(axis)
+    copies = []
+    for by in range(1, count):
+        peer = lax.rem(me + by, count)
+        copy = pltpu.make_async_remote_copy(
+            src_ref=source_of(peer),
+            dst_ref=target.at[me],
+            send_sem=send_sems.at[by],
+            recv_sem=recv_sems.at[by],
+            device_id={axis: peer},
+            device_id_type=pl.DeviceIdType.MESH,
+        )
+        copy.start()
+        copies.append(copy)
+    return copies
+
+
+def wait_all(copies):
+    for copy in copies:
+        copy.wait()
+
+
+def meet_peers(sizes):
+    barrier = pltpu.get_barrier_semaphore()
+    total = 0
+    for axis, count in sizes:
+        me = lax.axis_index(axis)
+        for by in range(1, count):
+            pl.semaphore_signal(
+                barrier,
+                inc=1,
+                device_id={axis: lax.rem(me + by, count)},
+                device_id_type=pl.DeviceIdType.MESH,
+            )
+        total += count - 1
+    pl.semaphore_wait(barrier, total)
+
+
+def head_kernel(
+    dp, loop, part_ref, mean_ref, rest_ref, pooled_ref, rest_out_ref, parts, own, sems
+):
+    meet_peers((("dp", dp), ("loop", loop)))
+    loop_me = lax.axis_index("loop")
+    dp_me = lax.axis_index("dp")
+    dp_copies = peer_copies(
+        "dp", dp, lambda peer: part_ref, parts, sems.at[0], sems.at[1]
+    )
+    rest_copies = peer_copies(
+        "loop", loop, lambda peer: rest_ref, rest_out_ref, sems.at[2], sems.at[3]
+    )
+    parts[dp_me] = part_ref[...]
+    rest_out_ref[loop_me] = rest_ref[...]
+    wait_all(dp_copies)
+    total = parts[0]
+    for at in range(1, dp):
+        total = total + parts[at]
+    own[...] = mean_ref[...] + total
+    pooled_copies = peer_copies(
+        "loop", loop, lambda peer: own, pooled_ref, sems.at[4], sems.at[5]
+    )
+    pooled_ref[loop_me] = own[...]
+    wait_all(rest_copies)
+    wait_all(pooled_copies)
+
+
+def head_exchange(part, mean, rest):
+    dp = lax.axis_size("dp")
+    loop = lax.axis_size("loop")
+    whole = pl.BlockSpec(memory_space=pltpu.VMEM)
+    return pl.pallas_call(
+        functools.partial(head_kernel, dp, loop),
+        out_shape=(
+            jax.ShapeDtypeStruct((loop,) + part.shape, jnp.float32),
+            jax.ShapeDtypeStruct((loop,) + rest.shape, jnp.float32),
         ),
-    )(padded, unit, inverse, gain, grad)
+        in_specs=[whole] * 3,
+        out_specs=(whole, whole),
+        scratch_shapes=[
+            pltpu.VMEM((dp,) + part.shape, jnp.float32),
+            pltpu.VMEM(part.shape, jnp.float32),
+            pltpu.SemaphoreType.DMA((6, max(dp, loop))),
+        ],
+        compiler_params=pltpu.CompilerParams(
+            collective_id=0, has_side_effects=True, vmem_limit_bytes=16 * 1024 * 1024
+        ),
+    )(part, mean, rest)
+
+
+def total_kernel(dp, loop, part_ref, out_ref, dp_slots, loop_slots, block, chunk, sems):
+    meet_peers((("dp", dp), ("loop", loop)))
+    loop_me = lax.axis_index("loop")
+    dp_me = lax.axis_index("dp")
+    copies = peer_copies(
+        "dp", dp, lambda peer: part_ref.at[peer], dp_slots, sems.at[0], sems.at[1]
+    )
+    dp_slots[dp_me] = part_ref[dp_me]
+    wait_all(copies)
+    total = dp_slots[0]
+    for at in range(1, dp):
+        total = total + dp_slots[at]
+    block[...] = total
+    copies = peer_copies(
+        "loop", loop, lambda peer: block.at[peer], loop_slots, sems.at[2], sems.at[3]
+    )
+    loop_slots[loop_me] = block[loop_me]
+    wait_all(copies)
+    total = loop_slots[0]
+    for at in range(1, loop):
+        total = total + loop_slots[at]
+    chunk[...] = total
+    mine = out_ref.at[dp_me]
+    copies = peer_copies("loop", loop, lambda peer: chunk, mine, sems.at[4], sems.at[5])
+    out_ref[dp_me, loop_me] = chunk[...]
+    wait_all(copies)
+    copies = peer_copies("dp", dp, lambda peer: mine, out_ref, sems.at[6], sems.at[7])
+    wait_all(copies)
+
+
+def total_sum(part):
+    dp = lax.axis_size("dp")
+    loop = lax.axis_size("loop")
+    rows = part.shape[0] * part.shape[1] // (dp * loop)
+    whole = pl.BlockSpec(memory_space=pltpu.VMEM)
+    summed = pl.pallas_call(
+        functools.partial(total_kernel, dp, loop),
+        out_shape=jax.ShapeDtypeStruct((dp, loop, rows, LANES), jnp.float32),
+        in_specs=[whole],
+        out_specs=whole,
+        scratch_shapes=[
+            pltpu.VMEM((dp, loop, rows, LANES), jnp.float32),
+            pltpu.VMEM((loop, rows, LANES), jnp.float32),
+            pltpu.VMEM((loop, rows, LANES), jnp.float32),
+            pltpu.VMEM((rows, LANES), jnp.float32),
+            pltpu.SemaphoreType.DMA((8, max(dp, loop))),
+        ],
+        compiler_params=pltpu.CompilerParams(
+            collective_id=1, has_side_effects=True, vmem_limit_bytes=32 * 1024 * 1024
+        ),
+    )(part.reshape(dp, loop, rows, LANES))
+    return summed.reshape(part.shape)
+
+
+def dense_rows(values):
+    return values.reshape(-1, LANES)
 
 
 def on_device(
@@ -235,9 +378,6 @@
 
     text_unit, text_inverse = unit_rows(text_embeds.astype(jnp.float32))
     cell_mean = jnp.mean(features.astype(jnp.float32), axis=(1, 2))
-    text_all = gather(text_unit)
-    mean_all = gather(cell_mean)
-    ids_all = lax.all_gather(image_ids, "loop", axis=0, tiled=True)
 
     padded = jnp.pad(
         features.astype(jnp.float32), ((0, 0), (0, 0), (0, ROWS - GRID), (0, 0))
@@ -258,12 +398,21 @@
     )
     slope = gelu_slope(pre_act)
     slope_all = gather(slope)
-    hidden_all = (gather(hidden_sum) / cell_count).astype(jnp.bfloat16)
+    hidden_own = (hidden_sum / cell_count).astype(jnp.bfloat16)
     mlp_part = lax.dot_general(
-        hidden_all, w_down, (((1,), (1,)), ((), ())), preferred_element_type=jnp.float32
-    )
-    mlp_pool = lax.psum(mlp_part, "dp")
-    pooled = (mean_all + mlp_pool).astype(jnp.bfloat16)
+        hidden_own, w_down, (((1,), (1,)), ((), ())), preferred_element_type=jnp.float32
+    )
+    id_row = jnp.pad(image_ids.astype(jnp.float32), (0, LANES - image_rows))[None, :]
+    rest = jnp.concatenate([dense_rows(hidden_sum), dense_rows(text_unit), id_row], axis=0)
+    hidden_rows = image_rows * hidden_share // LANES
+    text_end = hidden_rows + text_unit.size // LANES
+    rest = jnp.pad(rest, ((0, -rest.shape[0] % ROWS), (0, 0)))
+    pooled_all, rest_all = head_exchange(dense_rows(mlp_part), dense_rows(cell_mean), rest)
+    pooled = pooled_all.reshape(image_count, channels).astype(jnp.bfloat16)
+    hidden_all = rest_all[:, :hidden_rows].reshape(image_count, hidden_share)
+    hidden_all = (hidden_all / cell_count).astype(jnp.bfloat16)
+    text_all = rest_all[:, hidden_rows:text_end].reshape(-1, text_embeds.shape[1])
+    ids_all = rest_all[:, text_end, :image_rows].reshape(image_count).astype(jnp.int32)
     embedding = jnp.dot(pooled, projection, preferred_element_type=jnp.float32)
     image_unit, image_inverse = unit_rows(embedding)
     logits = (
@@ -298,7 +447,7 @@
         grad_pre, w_up, (((1,), (1,)), ((), ())), preferred_element_type=jnp.float32
     ).reshape(padded.shape)
     part = conv_grads(padded, unit, inverse, gain_row, grad_normed)
-    total = lax.psum(part, ("dp", "loop"))
+    total = total_sum(part).transpose(1, 0, 2).reshape(TAP_ROWS, channels)
     grad_kernel = total[:cell_count].reshape(GRID, GRID, channels)
     grad_bias = total[cell_count]
     grad_gain = total[cell_count + 1]

time: 322 us -> 167 us (0.52)
  waiting for transfers between devices: 181 us -> 0.04 us
  Pallas kernels: 12 us -> 102 us
  blocking collectives: 55.7 us -> 0 us
  local copies, waits for them, and re-layouts: 17.3 us -> 8.37 us
    psum x2 -> x0, waiting for transfers between devices: 122 us -> none  [the longest x1 122 us: on_device(): total = lax.psum(part, ('dp', 'loop'))]
    pallas_call x1 -> x3, Pallas kernels: 6.55 us -> 96.5 us  [the longest x1 76.1 us: total_sum(): pl.pallas_call(functools.partial(total_kernel, dp, loop), out_shape=jax.S...]
    all_gather x1, waiting for transfers between devices: 57.8 us -> 0.02 us  [on_device(): slope_all = gather(slope)]
    all_gather x3 -> x0, blocking collectives: 46.2 us -> none  [the longest x1 15.7 us: on_device(): hidden_all = (gather(hidden_sum) / cell_count).astype(jnp.bfloat16)]
    unnamed x1 -> x0, blocking collectives: 9.46 us -> none
    unnamed x44 -> x13, local copies, waits for them, and re-layouts: 7.99 us -> 1.24 us
  transfers between devices with their start and end apart: 4 -> 2, of which waited for: 2 -> 0; matrix products, arithmetic and copies ran while one was open for 6% -> 8% of each run, Pallas kernels for 0% -> 49%
where the time goes in v2:
time: 167 us
  Pallas kernels  102 us (61%)
  matrix products  24.9 us (15%)
  between operations  15.6 us (9%)
  other arithmetic  11.6 us (7%)
  local copies, waits for them, and re-layouts  8.37 us (5%)
  starting transfers between devices  4.33 us (3%)
    pallas_call x1, Pallas kernels, total_sum(): pl.pallas_call(functools.partial(total_kernel, dp, loop), out_shape=jax.S...  76.1 us
    pallas_call x1, Pallas kernels, head_exchange(): pl.pallas_call(functools.partial(head_kernel, dp, loop), out_shape=(jax.S...  14.7 us
    pallas_call x1, Pallas kernels, conv_grads(): pl.pallas_call(conv_grad_kernel, out_shape=jax.ShapeDtypeStruct((channels...  5.79 us
    pallas_call x1, Pallas kernels, conv_norm(): pl.pallas_call(conv_norm_kernel, out_shape=(full, jax.ShapeDtypeStruct((c...  5.41 us
    all_to_all x1, starting transfers between devices, on_device(): lax.all_to_all(unit_rows_own, 'loop', split_axis=1, concat_axis=0, tiled=...  4.29 us
    dot_general x1, matrix products, on_device(): lax.dot_general(grad_embed, projection, (((1,), (1,)), ((), ())), preferr...  4.17 us
    dot_general x1, matrix products, on_device(): lax.dot_general(grad_pre, w_up, (((1,), (1,)), ((), ())), preferred_eleme...  4.17 us
    dot_general x1, matrix products, on_device(): pre_act = jnp.dot(normed_rows, w_up, preferred_element_type=jnp.float32)  3.99 us
  transfers between devices with their start and end apart: 2, of which 0 were waited for; matrix products, arithmetic and copies ran while one was open for 8% of the time, Pallas kernels for 49%

profile of v2, /device:TPU:0, one launch (start us, length us, event | category | flops | bytes accessed | tf_op | source)
XLA Modules:
  0.0 166.9 jit_solution(5730982464128085788)
XLA Ops:
  7.2 0.0 all-gather.2.cloned.1.call-start
  7.2 1.9 %convert_reduce_fusion = f32[3,2048]{1,0:T(4,128)} fusion(bf16[3,7,7,2048]{3,2,1,0:T(8,128)(2,1)} %param.12), kind=kLoop, calls=%fused_computation.21 | loop fusion | flops 595968 | bytes 626688 | tf_op jit(solution)/shard_map/reduce_sum | solution.py:380
  9.1 1.2 pad.12.x_ref
  10.4 1.0 reshape.114.k_ref
  11.4 0.0 copy-start.1
  11.4 0.7 copy-done.1
  12.1 5.4 %shard_map.179 = (f32[3,7,8,2048]{3,2,1,0:T(8,128)S(1)}, f32[3,7,8,128]{3,2,1,0:T(8,128)S(1)}) custom-call(f32[3,7,8,2048]{3,2,1,0:T(8,128)S(1)} %pad.12.x_ref, f32[49,2048]{1,0:T(8,128)S(1)} %reshape.114.k_ref, f32[1,2048]{1,0:T(1,128)S(1)} %bitcast.66), custom_call_target="tpu_custom_call" | custom-call | tf_op jit(solution)/shard_map/pallas_call | solution.py:116
  17.5 0.1 fusion.4
  17.6 4.0 %multiply_multiply_fusion.1 = (f32[168,1024]{1,0:T(8,128)S(1)}, f32[168,1024]{1,0:T(8,128)}) fusion(bf16[168,2048]{1,0:T(8,128)(2,1)S(1)} %fusion.4, bf16[2048,1024]{1,0:T(8,128)(2,1)} %param.19), kind=kOutput, calls=%fused_computation.20 | convolution fusion | flops 705331200 | bytes 6258688 | tf_op jit(solution)/shard_map/dot_general | solution.py:395
  21.6 0.1 reduce_sum.63
  21.7 0.0 copy-start.4
  21.7 0.0 copy-start.5
  21.7 3.4 %fusion.26 = f32[3,2048]{1,0:T(4,128)S(1)} fusion(bf16[2048,1024]{1,0:T(8,128)(2,1)} %param.20, f32[3,1024]{1,0:T(4,128)S(1)} %reduce_sum.63), kind=kOutput, calls=%fused_computation.54 | convolution fusion | flops 12589056 | bytes 4231168 | tf_op jit(solution)/shard_map/dot_general | solution.py:402
  25.2 0.7 convert_element_type.64
  25.9 0.1 fusion.18
  26.0 0.1 convert_multiply_fusion
  26.1 14.7 %shard_map.180 = (f32[8,48,128]{2,1,0:T(8,128)S(1)}, f32[8,48,128]{2,1,0:T(8,128)S(1)}) custom-call(f32[48,128]{1,0:T(8,128)S(1)} %reshape.106.part_ref, f32[48,128]{1,0:T(8,128)S(1)} %div.27.mean_ref, f32[48,128]{1,0:T(8,128)S(1)} %select_maximum_fusion.rest_ref), custom_call_target="tpu_custom_call" | custom-call | tf_op jit(solution)/shard_map/pallas_call | solution.py:277
  41.5 0.1 convert_element_type.66
  42.3 0.7 convert_element_type.67
  42.9 0.9 convert_element_type.68
  43.9 3.2 %multiply_reduce_fusion.1 = (f32[24]{0:T(128)S(1)}, f32[24,1152]{1,0:T(8,128)S(1)}) fusion(bf16[24,2048]{1,0:T(8,128)(2,1)S(1)} %convert_element_type.68, bf16[2048,1152]{1,0:T(8,128)(2,1)} %param.21), kind=kOutput, calls=%fused_computation.24 | convolution fusion | flops 113301480 | bytes 4927584 | tf_op jit(solution)/shard_map/dot_general | solution.py:416
  47.1 0.3 fusion.20
  47.4 0.4 multiply_reduce_fusion
  47.8 0.1 multiply_convert_fusion
  47.9 4.2 %convolution_convert_fusion = bf16[24,2048]{1,0:T(8,128)(2,1)S(1)} fusion(bf16[24,1152]{1,0:T(8,128)(2,1)S(1)} %multiply_convert_fusion, bf16[2048,1152]{1,0:T(8,128)(2,1)} %param.21), kind=kOutput, calls=%fused_computation.4 | convolution fusion | flops 113295360 | bytes 4872192 | tf_op jit(solution)/shard_map/dot_general | solution.py:436
  52.1 0.0 copy-done.2
  52.1 0.7 convolution_multiply_fusion
  52.8 2.3 %fusion.10 = (bf16[168,1024]{1,0:T(8,128)(2,1)}, f32[168,1024]{1,0:T(8,128)}) fusion(f32[3,1024]{1,0:T(4,128)S(1)} %constant_dynamic-slice_fusion, f32[168,1024]{1,0:T(8,128)} %get-tuple-element.23), kind=kLoop, calls=%fused_computation.18 | loop fusion | flops 1720320 | bytes 1732608 | tf_op jit(solution)/shard_map/convert_element_type | solution.py:444
  55.2 0.0 all-gather.2.cloned.1.call-update
  55.2 0.5 copy.24
  55.7 1.5 copy.22
  57.2 4.3 %all-to-all-start = ((f32[168,8,256]{2,0,1:T(8,128)}), f32[168,8,256]{2,0,1:T(8,128)}, u32[]{:S(2)}, u32[]{:S(2)}) async-start(f32[168,8,256]{2,0,1:T(8,128)} %copy.22), calls=%async_computation | async-start | bytes 2752512 | tf_op jit(solution)/shard_map/all_to_all | solution.py:393
  61.5 0.6 dynamic_slice.18
  62.1 4.2 %fusion.1.grad_ref = f32[3,7,8,2048]{3,2,1,0:T(8,128)S(1)} fusion(bf16[3,7,8,1024]{3,2,1,0:T(8,128)(2,1)} %bitcast.69, bf16[2048,1024]{1,0:T(8,128)(2,1)} %param.19), kind=kOutput, calls=%fused_computation.2 | convolution fusion | flops 704643072 | bytes 5914624 | tf_op jit(solution)/shard_map/dot_general | solution.py:446
  66.3 5.8 %shard_map.181 = f32[16,64,128]{2,1,0:T(8,128)S(1)} custom-call(f32[3,7,8,2048]{3,2,1,0:T(8,128)S(1)} %pad.12.x_ref, f32[3,7,8,2048]{3,2,1,0:T(8,128)S(1)} %get-tuple-element.12.unit_ref, f32[3,7,8,128]{3,2,1,0:T(8,128)S(1)} %get-tuple-element.15.inv_ref, f32[1,2048]{1,0:T(1,128)S(1)} %bitcast.65, f32[3,7,8,2048]{3,2,1,0:T(8,128)S(1)} %fusion.1.grad_ref), custom_call_target="tpu_custom_call" | custom-call | tf_op jit(solution)/shard_map/pallas_call | solution.py:197
  72.1 76.1 %shard_map.182 = f32[4,8,32,128]{3,2,1,0:T(8,128)S(1)} custom-call(f32[4,8,32,128]{3,2,1,0:T(8,128)S(1)} %bitcast.62), custom_call_target="tpu_custom_call" | custom-call | tf_op jit(solution)/shard_map/pallas_call | solution.py:331
  148.2 0.1 copy.21
  148.3 0.8 reshape.112
  149.1 0.1 dynamic_slice.21
  149.2 0.6 fusion.37
  149.8 0.4 multiply_reduce_fusion.2
  150.2 1.0 fusion.29
  151.2 1.3 fusion.16
  152.5 0.7 subtract_multiply_fusion
  153.2 1.4 fusion.3
  154.6 0.0 all-gather.2.cloned.1.call-done
  154.7 3.4 %fusion = bf16[1344,1024]{1,0:T(8,128)(2,1)S(1)} fusion(f32[1344,1024]{1,0:T(8,128)} %all-gather.2.cloned.1.call-done, f32[24,1024]{1,0:T(8,128)S(1)} %convolution_multiply_fusion), kind=kLoop, calls=%fused_computation.1 | loop fusion | flops 2752512 | bytes 8355840 | tf_op jit(solution)/shard_map/convert_element_type | solution.py:469
  158.0 2.0 %fusion.38 = f32[256,1024]{1,0:T(8,128)} fusion(bf16[1344,256]{1,0:T(8,128)(2,1)S(1)} %fusion.3, bf16[1344,1024]{1,0:T(8,128)(2,1)S(1)} %fusion), kind=kOutput, calls=%fused_computation.70 | convolution fusion | flops 704643072 | bytes 4489216 | tf_op jit(solution)/shard_map/dot_general | solution.py:473
  (24 shorter events, 0.3 us)
Async XLA Ops:
  7.2 10.3 %copy-start = (f32[2048]{0:T(1024)S(1)}, f32[2048]{0:T(1024)}, u32[]{:S(2)}) copy-start(f32[2048]{0:T(1024)} %param.18) | copy-start | bytes 24580
  7.2 147.5 %all-gather.2.cloned.1.call-start = ((), (), s32[]{:S(2)}) async-start(), calls=%async_computation.1 | async-start | bytes 6193152 | tf_op jit(solution)/shard_map/all_gather | solution.py:400
  11.4 0.7 copy-start.1
  21.7 3.5 %copy-start.3 = (f32[3,2048]{1,0:T(4,128)S(1)}, f32[3,2048]{1,0:T(4,128)}, u32[]{:S(2)}) copy-start(f32[3,2048]{1,0:T(4,128)} %convert_reduce_fusion) | copy-start | bytes 73732
  21.7 4.2 %copy-start.4 = (bf16[2,1152]{1,0:T(2,128)(2,1)S(1)}, bf16[2,1152]{1,0:T(2,128)(2,1)}, u32[]{:S(2)}) copy-start(bf16[2,1152]{1,0:T(2,128)(2,1)} %param.14) | copy-start | bytes 13828
  21.7 25.4 %copy-start.5 = (s32[16]{0:T(128)S(1)}, s32[16]{0:T(128)}, u32[]{:S(2)}) copy-start(s32[16]{0:T(128)} %param.15) | copy-start | bytes 196
  47.1 5.1 %copy-start.2 = (bf16[2048,1024]{1,0:T(8,128)(2,1)S(1)}, bf16[2048,1024]{1,0:T(8,128)(2,1)}, u32[]{:S(2)}) copy-start(bf16[2048,1024]{1,0:T(8,128)(2,1)} %param.20) | copy-start | bytes 12582916
  57.2 96.0 %all-to-all-start = ((f32[168,8,256]{2,0,1:T(8,128)}), f32[168,8,256]{2,0,1:T(8,128)}, u32[]{:S(2)}, u32[]{:S(2)}) async-start(f32[168,8,256]{2,0,1:T(8,128)} %copy.22), calls=%async_computation | async-start | bytes 2752512 | tf_op jit(solution)/shard_map/all_to_all | solution.py:393
Sparse Core Ops, SparseCore 0:
  55.3 91.1 all-gather.1

commit v3 on v2

--- a/solution.py
+++ b/solution.py
@@ -287,6 +287,7 @@
             pltpu.VMEM(part.shape, jnp.float32),
             pltpu.SemaphoreType.DMA((6, max(dp, loop))),
         ],
+        cost_estimate=pl.CostEstimate(flops=1000, bytes_accessed=1000, transcendentals=0),
         compiler_params=pltpu.CompilerParams(
             collective_id=0, has_side_effects=True, vmem_limit_bytes=16 * 1024 * 1024
         ),
@@ -437,6 +438,7 @@
         grad_embed, projection, (((1,), (1,)), ((), ())), preferred_element_type=jnp.float32
     ).astype(jnp.bfloat16)
     spread = jnp.dot(grad_pooled, w_down, preferred_element_type=jnp.float32) / cell_count
+    spread, slope_all, unit_share = lax.optimization_barrier((spread, slope_all, unit_share))
     own_spread = lax.dynamic_slice_in_dim(spread, first_image, image_rows)
     grad_pre = (
         (slope.reshape(image_rows, GRID * ROWS, hidden_share) * own_spread[:, None, :])

time: 167 us -> 185 us (1.11)
  Pallas kernels: 102 us -> 119 us
  other arithmetic: 11.6 us -> 6.64 us
  matrix products: 24.9 us -> 27 us
  starting transfers between devices: 4.33 us -> 6.38 us
    pallas_call x1, Pallas kernels: 14.7 us -> 79.1 us  [head_exchange(): pl.pallas_call(functools.partial(head_kernel, dp, loop), out_shape=(jax.S...]
    pallas_call x1, Pallas kernels: 76.1 us -> 28.9 us  [total_sum(): pl.pallas_call(functools.partial(total_kernel, dp, loop), out_shape=jax.S...]
    convert_element_type x1, other arithmetic: 2.34 us -> 0.06 us  [on_device(): grad_pre = (slope.reshape(image_rows, GRID * ROWS, hidden_share) * own_sp...]
    all_to_all x1, starting transfers between devices: 4.29 us -> 6.34 us  [on_device(): lax.all_to_all(unit_rows_own, 'loop', split_axis=1, concat_axis=0, tiled=...]
  transfers between devices with their start and end apart: 2 -> 2, of which waited for: 0 -> 0; matrix products, arithmetic and copies ran while one was open for 8% -> 13% of each run, Pallas kernels for 49% -> 43%
where the time goes in v3:
time: 185 us
  Pallas kernels  119 us (64%)
  matrix products  27 us (15%)
  between operations  15.6 us (8%)
  local copies, waits for them, and re-layouts  9.83 us (5%)
  other arithmetic  6.64 us (4%)
  starting transfers between devices  6.38 us (3%)
    pallas_call x1, Pallas kernels, head_exchange(): pl.pallas_call(functools.partial(head_kernel, dp, loop), out_shape=(jax.S...  79.1 us
    pallas_call x1, Pallas kernels, total_sum(): pl.pallas_call(functools.partial(total_kernel, dp, loop), out_shape=jax.S...  28.9 us
    all_to_all x1, starting transfers between devices, on_device(): lax.all_to_all(unit_rows_own, 'loop', split_axis=1, concat_axis=0, tiled=...  6.34 us
    pallas_call x1, Pallas kernels, conv_grads(): pl.pallas_call(conv_grad_kernel, out_shape=jax.ShapeDtypeStruct((channels...  5.75 us
    pallas_call x1, Pallas kernels, conv_norm(): pl.pallas_call(conv_norm_kernel, out_shape=(full, jax.ShapeDtypeStruct((c...  5.36 us
    dot_general x1, matrix products, on_device(): pre_act = jnp.dot(normed_rows, w_up, preferred_element_type=jnp.float32)  4.18 us
    dot_general x1, matrix products, on_device(): lax.dot_general(grad_embed, projection, (((1,), (1,)), ((), ())), preferr...  3.86 us
    dot_general x1, matrix products, on_device(): lax.dot_general(grad_pre, w_up, (((1,), (1,)), ((), ())), preferred_eleme...  3.72 us
  transfers between devices with their start and end apart: 2, of which 0 were waited for; matrix products, arithmetic and copies ran while one was open for 13% of the time, Pallas kernels for 43%

profile of v3, /device:TPU:0, one launch (start us, length us, event | category | flops | bytes accessed | tf_op | source)
XLA Modules:
  0.0 184.5 jit_solution(15161308292801925946)
XLA Ops:
  7.2 0.0 all-gather.2.cloned.1.call-start
  7.2 1.0 reshape.114.k_ref
  8.2 1.2 pad.12.x_ref
  9.5 0.0 copy-start.1
  9.5 0.7 copy-done.1
  10.2 5.4 %shard_map.179 = (f32[3,7,8,2048]{3,2,1,0:T(8,128)S(1)}, f32[3,7,8,128]{3,2,1,0:T(8,128)S(1)}) custom-call(f32[3,7,8,2048]{3,2,1,0:T(8,128)S(1)} %pad.12.x_ref, f32[49,2048]{1,0:T(8,128)S(1)} %reshape.114.k_ref, f32[1,2048]{1,0:T(1,128)S(1)} %bitcast.62), custom_call_target="tpu_custom_call" | custom-call | tf_op jit(solution)/shard_map/pallas_call | solution.py:116
  15.6 0.1 fusion.3
  15.7 4.2 %fusion.8 = (f32[168,1024]{1,0:T(8,128)}, f32[168,1024]{1,0:T(8,128)S(1)}) fusion(bf16[168,2048]{1,0:T(8,128)(2,1)S(1)} %fusion.3, bf16[2048,1024]{1,0:T(8,128)(2,1)} %param.19), kind=kOutput, calls=%fused_computation.15 | convolution fusion | flops 706363392 | bytes 6258688 | tf_op jit(solution)/shard_map/dot_general | solution.py:396
  19.9 0.0 all-gather.2.cloned.1.call-update
  19.9 0.1 reduce_sum.63
  20.0 0.0 copy-start.6
  20.0 3.4 %fusion.27 = f32[3,2048]{1,0:T(4,128)S(1)} fusion(bf16[2048,1024]{1,0:T(8,128)(2,1)} %param.20, f32[3,1024]{1,0:T(4,128)S(1)} %reduce_sum.63), kind=kOutput, calls=%fused_computation.55 | convolution fusion | flops 12589056 | bytes 4231168 | tf_op jit(solution)/shard_map/dot_general | solution.py:403
  23.4 1.3 convert_reduce_fusion
  24.8 0.1 fusion.19
  24.9 0.1 convert_multiply_fusion
  25.0 0.5 copy.24
  25.5 1.5 copy.21
  27.0 0.0 copy-start.8
  27.0 6.3 %all-to-all-start = ((f32[168,8,256]{2,0,1:T(8,128)}), f32[168,8,256]{2,0,1:T(8,128)}, u32[]{:S(2)}, u32[]{:S(2)}) async-start(f32[168,8,256]{2,0,1:T(8,128)} %copy.21), calls=%async_computation | async-start | bytes 2752512 | tf_op jit(solution)/shard_map/all_to_all | solution.py:394
  33.4 79.1 %shard_map.180 = (f32[8,48,128]{2,1,0:T(8,128)S(1)}, f32[8,48,128]{2,1,0:T(8,128)S(1)}) custom-call(f32[48,128]{1,0:T(8,128)S(1)} %reshape.106.part_ref, f32[48,128]{1,0:T(8,128)S(1)} %div.27.mean_ref, f32[48,128]{1,0:T(8,128)S(1)} %select_maximum_fusion.rest_ref), custom_call_target="tpu_custom_call" | custom-call | flops 1000 | bytes 1000 | tf_op jit(solution)/shard_map/pallas_call | solution.py:277
  113.1 0.1 convert_element_type.66
  113.9 0.7 convert_element_type.67
  114.6 0.9 convert_element_type.68
  115.5 3.2 %multiply_reduce_fusion.1 = (f32[24]{0:T(128)S(1)}, f32[24,1152]{1,0:T(8,128)S(1)}) fusion(bf16[24,2048]{1,0:T(8,128)(2,1)S(1)} %convert_element_type.68, bf16[2048,1152]{1,0:T(8,128)(2,1)} %param.21), kind=kOutput, calls=%fused_computation.25 | convolution fusion | flops 113301480 | bytes 4927584 | tf_op jit(solution)/shard_map/dot_general | solution.py:417
  118.8 0.3 fusion.21
  119.1 0.9 multiply_reduce_fusion.2
  120.0 0.1 dynamic_slice.21
  120.1 0.6 convert_element_type.75
  120.7 0.6 dynamic_slice.18
  121.3 0.4 multiply_reduce_fusion
  121.7 0.1 multiply_convert_fusion.2
  121.8 1.0 fusion.30
  122.8 3.9 %convolution_convert_fusion = bf16[24,2048]{1,0:T(8,128)(2,1)S(1)} fusion(bf16[24,1152]{1,0:T(8,128)(2,1)S(1)} %multiply_convert_fusion.2, bf16[2048,1152]{1,0:T(8,128)(2,1)} %param.21), kind=kOutput, calls=%fused_computation.4 | convolution fusion | flops 113295360 | bytes 4872192 | tf_op jit(solution)/shard_map/dot_general | solution.py:437
  126.7 0.0 copy-done.5
  126.7 1.3 fusion.17
  128.0 1.3 convolution_multiply_fusion
  129.4 0.7 subtract_multiply_fusion
  130.0 0.0 all-to-all-done
  130.1 0.8 constant_dynamic-slice_fusion
  130.9 0.1 fusion.10
  131.0 3.7 %fusion.1.grad_ref = f32[3,7,8,2048]{3,2,1,0:T(8,128)S(1)} fusion(bf16[3,7,8,1024]{3,2,1,0:T(8,128)(2,1)S(1)} %bitcast.65, bf16[2048,1024]{1,0:T(8,128)(2,1)} %param.19), kind=kOutput, calls=%fused_computation.2 | convolution fusion | flops 704643072 | bytes 5914624 | tf_op jit(solution)/shard_map/dot_general | solution.py:448
  134.7 5.7 %shard_map.181 = f32[16,64,128]{2,1,0:T(8,128)S(1)} custom-call(f32[3,7,8,2048]{3,2,1,0:T(8,128)S(1)} %pad.12.x_ref, f32[3,7,8,2048]{3,2,1,0:T(8,128)S(1)} %get-tuple-element.15.unit_ref, f32[3,7,8,128]{3,2,1,0:T(8,128)S(1)} %get-tuple-element.18.inv_ref, f32[1,2048]{1,0:T(1,128)S(1)} %bitcast.61, f32[3,7,8,2048]{3,2,1,0:T(8,128)S(1)} %fusion.1.grad_ref), custom_call_target="tpu_custom_call" | custom-call | tf_op jit(solution)/shard_map/pallas_call | solution.py:197
  140.5 28.9 %shard_map.182 = f32[4,8,32,128]{3,2,1,0:T(8,128)S(1)} custom-call(f32[4,8,32,128]{3,2,1,0:T(8,128)S(1)} %bitcast.58), custom_call_target="tpu_custom_call" | custom-call | tf_op jit(solution)/shard_map/pallas_call | solution.py:332
  169.4 0.6 fusion.37
  170.0 0.1 copy.22
  170.1 0.8 reshape.112
  171.0 3.4 %fusion = bf16[1344,1024]{1,0:T(8,128)(2,1)S(1)} fusion(f32[1344,1024]{1,0:T(8,128)} %all-gather.2.cloned.1.call-done, f32[24,1024]{1,0:T(8,128)S(1)} %copy-done.4), kind=kLoop, calls=%fused_computation.1 | loop fusion | flops 2752512 | bytes 8355840 | tf_op jit(solution)/shard_map/convert_element_type | solution.py:471
  174.4 3.3 %fusion.9 = f32[256,1024]{1,0:T(8,128)} fusion(bf16[1344,1024]{1,0:T(8,128)(2,1)S(1)} %fusion, f32[1344,256]{1,0:T(8,128)} %bitcast.8, f32[256]{0:T(256)S(1)} %dynamic_slice.21), kind=kOutput, calls=%fused_computation.16 | convolution fusion | flops 705331200 | bytes 5178368 | tf_op jit(solution)/shard_map/dot_general | solution.py:475
  (33 shorter events, 0.3 us)
Async XLA Ops:
  7.2 8.4 %copy-start = (f32[2048]{0:T(1024)S(1)}, f32[2048]{0:T(1024)}, u32[]{:S(2)}) copy-start(f32[2048]{0:T(1024)} %param.18) | copy-start | bytes 24580
  7.2 122.9 %all-gather.2.cloned.1.call-start = ((), (), s32[]{:S(2)}) async-start(), calls=%async_computation.1 | async-start | bytes 6193152 | tf_op jit(solution)/shard_map/all_gather | solution.py:401
  9.5 0.7 copy-start.1
  19.9 4.9 %copy-start.10 = (s32[3]{0:T(128)S(1)}, s32[3]{0:T(128)}, u32[]{:S(2)}) copy-start(s32[3]{0:T(128)} %param.13) | copy-start | bytes 40
  20.0 4.8 %copy-start.6 = (bf16[2,1152]{1,0:T(2,128)(2,1)S(1)}, bf16[2,1152]{1,0:T(2,128)(2,1)}, u32[]{:S(2)}) copy-start(bf16[2,1152]{1,0:T(2,128)(2,1)} %param.14) | copy-start | bytes 13828
  27.0 91.8 %copy-start.8 = (s32[16]{0:T(128)S(1)}, s32[16]{0:T(128)}, u32[]{:S(2)}) copy-start(s32[16]{0:T(128)} %param.15) | copy-start | bytes 196
  27.0 103.0 %all-to-all-start = ((f32[168,8,256]{2,0,1:T(8,128)}), f32[168,8,256]{2,0,1:T(8,128)}, u32[]{:S(2)}, u32[]{:S(2)}) async-start(f32[168,8,256]{2,0,1:T(8,128)} %copy.21), calls=%async_computation | async-start | bytes 2752512 | tf_op jit(solution)/shard_map/all_to_all | solution.py:394
  121.3 5.4 %copy-start.5 = (bf16[24,1024]{1,0:T(8,128)(2,1)S(1)}, bf16[24,1024]{1,0:T(8,128)(2,1)}, u32[]{:S(2)}) copy-start(bf16[24,1024]{1,0:T(8,128)(2,1)} %convert_element_type.75) | copy-start | bytes 147460
  121.3 6.7 %copy-start.2 = (bf16[2048,1024]{1,0:T(8,128)(2,1)S(1)}, bf16[2048,1024]{1,0:T(8,128)(2,1)}, u32[]{:S(2)}) copy-start(bf16[2048,1024]{1,0:T(8,128)(2,1)} %param.20) | copy-start | bytes 12582916
  122.8 6.5 %copy-start.7 = (bf16[2,1152]{1,0:T(2,128)(2,1)S(1)}, bf16[2,1152]{1,0:T(2,128)(2,1)}, u32[]{:S(2)}) copy-start(bf16[2,1152]{1,0:T(2,128)(2,1)} %param.14) | copy-start | bytes 13828
  122.8 6.5 %copy-start.9 = (f32[2]{0:T(128)S(1)}, f32[2]{0:T(128)}, u32[]{:S(2)}) copy-start(f32[2]{0:T(128)} %get-tuple-element.30) | copy-start | bytes 28
  122.8 8.1 %copy-start.3 = (f32[168,1024]{1,0:T(8,128)S(1)}, f32[168,1024]{1,0:T(8,128)}, u32[]{:S(2)}) copy-start(f32[168,1024]{1,0:T(8,128)} %get-tuple-element.22) | copy-start | bytes 2064388
  134.7 36.3 %copy-start.4 = (f32[24,1024]{1,0:T(8,128)S(1)}, f32[24,1024]{1,0:T(8,128)}, u32[]{:S(2)}) copy-start(f32[24,1024]{1,0:T(8,128)} %convolution_multiply_fusion) | copy-start | bytes 294916
Sparse Core Ops, SparseCore 0:
  20.0 98.3 all-gather.1

commit v4 on v2

--- a/solution.py
+++ b/solution.py
@@ -397,7 +397,6 @@
         gelu_value(pre_act).reshape(image_rows, GRID * ROWS, hidden_share), axis=1
     )
     slope = gelu_slope(pre_act)
-    slope_all = gather(slope)
     hidden_own = (hidden_sum / cell_count).astype(jnp.bfloat16)
     mlp_part = lax.dot_general(
         hidden_own, w_down, (((1,), (1,)), ((), ())), preferred_element_type=jnp.float32
@@ -408,6 +407,8 @@
     text_end = hidden_rows + text_unit.size // LANES
     rest = jnp.pad(rest, ((0, -rest.shape[0] % ROWS), (0, 0)))
     pooled_all, rest_all = head_exchange(dense_rows(mlp_part), dense_rows(cell_mean), rest)
+    slope_sent, unit_share, pooled_all = lax.optimization_barrier((slope, unit_share, pooled_all))
+    slope_all = gather(slope_sent)
     pooled = pooled_all.reshape(image_count, channels).astype(jnp.bfloat16)
     hidden_all = rest_all[:, :hidden_rows].reshape(image_count, hidden_share)
     hidden_all = (hidden_all / cell_count).astype(jnp.bfloat16)

time: 167 us -> 143 us (0.86)
  Pallas kernels: 102 us -> 74.3 us
  other arithmetic: 11.6 us -> 5.93 us
  waiting for transfers between devices: 0.04 us -> 5.52 us
  starting transfers between devices: 4.33 us -> 6.36 us
    pallas_call x1, Pallas kernels: 76.1 us -> 31.3 us  [total_sum(): pl.pallas_call(functools.partial(total_kernel, dp, loop), out_shape=jax.S...]
    pallas_call x1, Pallas kernels: 14.7 us -> 31.9 us  [head_exchange(): pl.pallas_call(functools.partial(head_kernel, dp, loop), out_shape=(jax.S...]
    all_gather x1, waiting for transfers between devices: 0.02 us -> 5.51 us  [on_device(): slope_all = gather(slope_sent)]
    dot_general x1, matrix products: 4.17 us -> 1.54 us  [on_device(): lax.dot_general(grad_pre, w_up, (((1,), (1,)), ((), ())), preferred_eleme...]
    convert_element_type x1, other arithmetic: 2.34 us -> 0.06 us  [on_device(): grad_pre = (slope.reshape(image_rows, GRID * ROWS, hidden_share) * own_sp...]
    all_to_all x1, starting transfers between devices: 4.29 us -> 6.33 us  [on_device(): lax.all_to_all(unit_rows_own, 'loop', split_axis=1, concat_axis=0, tiled=...]
  transfers between devices with their start and end apart: 2 -> 2, of which waited for: 0 -> 1; matrix products, arithmetic and copies ran while one was open for 8% -> 20% of each run, Pallas kernels for 49% -> 48%
where the time goes in v4:
time: 143 us; the launch traced here: 142 us
  Pallas kernels  74.3 us (52%)
  matrix products  25.7 us (18%)
  between operations  15.8 us (11%)
  local copies, waits for them, and re-layouts  8.7 us (6%)
  starting transfers between devices  6.36 us (4%)
  other arithmetic  5.93 us (4%)
  waiting for transfers between devices  5.52 us (4%)
    pallas_call x1, Pallas kernels, head_exchange(): pl.pallas_call(functools.partial(head_kernel, dp, loop), out_shape=(jax.S...  31.9 us
    pallas_call x1, Pallas kernels, total_sum(): pl.pallas_call(functools.partial(total_kernel, dp, loop), out_shape=jax.S...  31.3 us
    all_to_all x1, starting transfers between devices, on_device(): lax.all_to_all(unit_rows_own, 'loop', split_axis=1, concat_axis=0, tiled=...  6.33 us
    pallas_call x1, Pallas kernels, conv_grads(): pl.pallas_call(conv_grad_kernel, out_shape=jax.ShapeDtypeStruct((channels...  5.76 us
    all_gather x1, waiting for transfers between devices, on_device(): slope_all = gather(slope_sent)  5.51 us
    pallas_call x1, Pallas kernels, conv_norm(): pl.pallas_call(conv_norm_kernel, out_shape=(full, jax.ShapeDtypeStruct((c...  5.36 us
    dot_general x1, matrix products, on_device(): lax.dot_general(grad_embed, projection, (((1,), (1,)), ((), ())), preferr...  4.43 us
    dot_general x1, matrix products, on_device(): pre_act = jnp.dot(normed_rows, w_up, preferred_element_type=jnp.float32)  4.18 us
  transfers between devices with their start and end apart: 2, of which 1 were waited for; matrix products, arithmetic and copies ran while one was open for 20% of the time, Pallas kernels for 48%

profile of v4, /device:TPU:0, one launch (start us, length us, event | category | flops | bytes accessed | tf_op | source)
XLA Modules:
  0.0 142.2 jit_solution(3565344948574005815)
XLA Ops:
  7.2 1.0 reshape.114.k_ref
  8.2 1.2 pad.12.x_ref
  9.4 0.0 copy-start.1
  9.4 0.7 copy-done.1
  10.1 5.4 %shard_map.179 = (f32[3,7,8,2048]{3,2,1,0:T(8,128)S(1)}, f32[3,7,8,128]{3,2,1,0:T(8,128)S(1)}) custom-call(f32[3,7,8,2048]{3,2,1,0:T(8,128)S(1)} %pad.12.x_ref, f32[49,2048]{1,0:T(8,128)S(1)} %reshape.114.k_ref, f32[1,2048]{1,0:T(1,128)S(1)} %bitcast.62), custom_call_target="tpu_custom_call" | custom-call | tf_op jit(solution)/shard_map/pallas_call | solution.py:116
  15.5 0.0 copy-start
  15.5 0.5 copy.24
  16.0 1.5 %copy.21 = f32[168,8,256]{2,0,1:T(8,128)} copy(f32[168,8,256]{2,1,0:T(8,128)S(1)} %bitcast.63) | data formatting | bytes 2752512 | tf_op jit(solution)/shard_map/all_to_all | solution.py:393
  17.5 6.3 %all-to-all-start = ((f32[168,8,256]{2,0,1:T(8,128)}), f32[168,8,256]{2,0,1:T(8,128)}, u32[]{:S(2)}, u32[]{:S(2)}) async-start(f32[168,8,256]{2,0,1:T(8,128)} %copy.21), calls=%async_computation | async-start | bytes 2752512 | tf_op jit(solution)/shard_map/all_to_all | solution.py:393
  23.9 0.0 all-gather.2.cloned.1.call-start
  23.9 0.1 fusion.3
  24.0 4.2 %fusion.8 = (f32[168,1024]{1,0:T(8,128)}, f32[168,1024]{1,0:T(8,128)S(1)}) fusion(bf16[168,2048]{1,0:T(8,128)(2,1)S(1)} %fusion.3, bf16[2048,1024]{1,0:T(8,128)(2,1)} %param.19), kind=kOutput, calls=%fused_computation.15 | convolution fusion | flops 706363392 | bytes 6258688 | tf_op jit(solution)/shard_map/dot_general | solution.py:395
  28.2 0.1 reduce_sum.63
  28.3 3.4 %fusion.27 = f32[3,2048]{1,0:T(4,128)S(1)} fusion(bf16[2048,1024]{1,0:T(8,128)(2,1)} %param.20, f32[3,1024]{1,0:T(4,128)S(1)} %reduce_sum.63), kind=kOutput, calls=%fused_computation.55 | convolution fusion | flops 12589056 | bytes 4231168 | tf_op jit(solution)/shard_map/dot_general | solution.py:401
  31.7 1.3 convert_reduce_fusion
  33.1 0.1 fusion.19
  33.2 0.1 convert_multiply_fusion
  33.3 31.9 %shard_map.180 = (f32[8,48,128]{2,1,0:T(8,128)S(1)}, f32[8,48,128]{2,1,0:T(8,128)S(1)}) custom-call(f32[48,128]{1,0:T(8,128)S(1)} %reshape.106.part_ref, f32[48,128]{1,0:T(8,128)S(1)} %div.27.mean_ref, f32[48,128]{1,0:T(8,128)S(1)} %select_maximum_fusion.rest_ref), custom_call_target="tpu_custom_call" | custom-call | tf_op jit(solution)/shard_map/pallas_call | solution.py:277
  65.2 0.0 all-gather.2.cloned.1.call-update
  66.0 0.1 convert_element_type.66
  66.7 0.1 dynamic_slice.21
  66.8 0.6 convert_element_type.75
  67.5 0.0 copy-start.11
  67.6 3.3 %multiply_reduce_fusion.1 = (f32[24]{0:T(128)S(1)}, f32[24,1152]{1,0:T(8,128)S(1)}) fusion(bf16[24,2048]{1,0:T(8,128)(2,1)S(1)} %convert_element_type.68, bf16[2048,1152]{1,0:T(8,128)(2,1)} %param.21), kind=kOutput, calls=%fused_computation.25 | convolution fusion | flops 113301480 | bytes 4927584 | tf_op jit(solution)/shard_map/dot_general | solution.py:417
  70.9 0.0 copy-start.4
  70.9 0.3 fusion.21
  71.3 0.6 dynamic_slice.18
  71.9 0.4 multiply_reduce_fusion
  72.3 0.1 multiply_convert_fusion.2
  72.4 4.4 %convolution_convert_fusion = bf16[24,2048]{1,0:T(8,128)(2,1)S(1)} fusion(bf16[24,1152]{1,0:T(8,128)(2,1)S(1)} %multiply_convert_fusion.2, bf16[2048,1152]{1,0:T(8,128)(2,1)} %param.21), kind=kOutput, calls=%fused_computation.4 | convolution fusion | flops 113295360 | bytes 4872192 | tf_op jit(solution)/shard_map/dot_general | solution.py:437
  76.8 0.0 copy-done.2
  76.9 0.7 convolution_multiply_fusion
  77.6 0.1 fusion.10
  77.7 0.5 copy-done.8
  78.2 1.5 %fusion.1.grad_ref = f32[3,7,8,2048]{3,2,1,0:T(8,128)S(1)} fusion(bf16[3,7,8,1024]{3,2,1,0:T(8,128)(2,1)S(1)} %bitcast.65, bf16[2048,1024]{1,0:T(8,128)(2,1)S(1)} %copy-done.16), kind=kOutput, calls=%fused_computation.2 | convolution fusion | flops 704643072 | bytes 5914624 | tf_op jit(solution)/shard_map/dot_general | solution.py:447
  79.8 0.0 copy-start.14
  79.8 5.8 %shard_map.181 = f32[16,64,128]{2,1,0:T(8,128)S(1)} custom-call(f32[3,7,8,2048]{3,2,1,0:T(8,128)S(1)} %pad.12.x_ref, f32[3,7,8,2048]{3,2,1,0:T(8,128)S(1)} %get-tuple-element.15.unit_ref, f32[3,7,8,128]{3,2,1,0:T(8,128)S(1)} %get-tuple-element.19.inv_ref, f32[1,2048]{1,0:T(1,128)S(1)} %bitcast.61, f32[3,7,8,2048]{3,2,1,0:T(8,128)S(1)} %fusion.1.grad_ref), custom_call_target="tpu_custom_call" | custom-call | tf_op jit(solution)/shard_map/pallas_call | solution.py:197
  85.6 31.3 %shard_map.182 = f32[4,8,32,128]{3,2,1,0:T(8,128)S(1)} custom-call(f32[4,8,32,128]{3,2,1,0:T(8,128)S(1)} %bitcast.58), custom_call_target="tpu_custom_call" | custom-call | tf_op jit(solution)/shard_map/pallas_call | solution.py:331
  116.9 0.1 copy.22
  117.0 0.8 reshape.112
  117.8 0.6 fusion.37
  118.4 0.4 multiply_reduce_fusion.2
  118.8 1.7 %fusion.30 = f32[64,1152]{1,0:T(8,128)} fusion(bf16[24,1152]{1,0:T(8,128)(2,1)S(1)} %copy-done.7, bf16[24,2048]{1,0:T(8,128)(2,1)} %copy-done.11, s32[]{:T(128)S(6)} %select_n.28), kind=kOutput, calls=%fused_computation.58 | convolution fusion | flops 3538944 | bytes 356356 | tf_op jit(solution)/shard_map/dot_general | solution.py:464
  120.5 2.0 %fusion.17 = f32[256,1024]{1,0:T(8,128)} fusion(bf16[24,1024]{1,0:T(8,128)(2,1)S(1)} %copy-done.12, bf16[24,2048]{1,0:T(8,128)(2,1)} %copy-done.10, s32[]{:T(128)S(6)} %select_n.27), kind=kOutput, calls=%fused_computation.41 | convolution fusion | flops 12582912 | bytes 1110020 | tf_op jit(solution)/shard_map/dot_general | solution.py:458
  122.5 0.7 subtract_multiply_fusion
  123.2 5.5 %all-gather.2.cloned.1.call-done = f32[1344,1024]{1,0:T(8,128)} async-done(((f32[168,1024]{1,0:T(8,128)}), f32[1344,1024]{1,0:T(8,128)}) %all-gather.2.cloned.1.call-update) | async-done | bytes 5505040 | tf_op jit(solution)/shard_map/all_gather | solution.py:411
  128.7 3.4 %fusion = bf16[1344,1024]{1,0:T(8,128)(2,1)S(1)} fusion(f32[1344,1024]{1,0:T(8,128)} %all-gather.2.cloned.1.call-done, f32[24,1024]{1,0:T(8,128)S(1)} %copy-done.9), kind=kLoop, calls=%fused_computation.1 | loop fusion | flops 2752512 | bytes 8355840 | tf_op jit(solution)/shard_map/convert_element_type | solution.py:470
  132.0 3.3 %fusion.9 = f32[256,1024]{1,0:T(8,128)} fusion(bf16[1344,1024]{1,0:T(8,128)(2,1)S(1)} %fusion, f32[1344,256]{1,0:T(8,128)} %bitcast.6, f32[256]{0:T(256)S(1)} %dynamic_slice.21), kind=kOutput, calls=%fused_computation.16 | convolution fusion | flops 705331200 | bytes 5178368 | tf_op jit(solution)/shard_map/dot_general | solution.py:474
  (47 shorter events, 0.4 us)
Async XLA Ops:
  9.4 0.7 copy-start.1
  15.5 8.4 %copy-start = (f32[2048]{0:T(1024)S(1)}, f32[2048]{0:T(1024)}, u32[]{:S(2)}) copy-start(f32[2048]{0:T(1024)} %param.18) | copy-start | bytes 24580
  17.5 47.7 %all-to-all-start = ((f32[168,8,256]{2,0,1:T(8,128)}), f32[168,8,256]{2,0,1:T(8,128)}, u32[]{:S(2)}, u32[]{:S(2)}) async-start(f32[168,8,256]{2,0,1:T(8,128)} %copy.21), calls=%async_computation | async-start | bytes 2752512 | tf_op jit(solution)/shard_map/all_to_all | solution.py:393
  23.9 104.8 %all-gather.2.cloned.1.call-start = ((), (), s32[]{:S(2)}) async-start(), calls=%async_computation.1 | async-start | bytes 6193152 | tf_op jit(solution)/shard_map/all_gather | solution.py:411
  28.2 4.8 %copy-start.17 = (s32[3]{0:T(128)S(1)}, s32[3]{0:T(128)}, u32[]{:S(2)}) copy-start(s32[3]{0:T(128)} %param.13) | copy-start | bytes 40
  28.3 4.8 %copy-start.13 = (bf16[2,1152]{1,0:T(2,128)(2,1)S(1)}, bf16[2,1152]{1,0:T(2,128)(2,1)}, u32[]{:S(2)}) copy-start(bf16[2,1152]{1,0:T(2,128)(2,1)} %param.14) | copy-start | bytes 13828
  31.7 39.2 %copy-start.15 = (s32[16]{0:T(128)S(1)}, s32[16]{0:T(128)}, u32[]{:S(2)}) copy-start(s32[16]{0:T(128)} %param.15) | copy-start | bytes 196
  67.5 4.7 %copy-start.11 = (bf16[24,2048]{1,0:T(8,128)(2,1)}, bf16[24,2048]{1,0:T(8,128)(2,1)S(1)}, u32[]{:S(2)}) copy-start(bf16[24,2048]{1,0:T(8,128)(2,1)S(1)} %convert_element_type.68) | copy-start | bytes 294916
  67.5 9.3 %copy-start.2 = (bf16[2048,1024]{1,0:T(8,128)(2,1)S(1)}, bf16[2048,1024]{1,0:T(8,128)(2,1)}, u32[]{:S(2)}) copy-start(bf16[2048,1024]{1,0:T(8,128)(2,1)} %param.20) | copy-start | bytes 12582916
  70.9 1.4 copy-start.4
  72.4 5.2 %copy-start.6 = (bf16[24,1152]{1,0:T(8,128)(2,1)}, bf16[24,1152]{1,0:T(8,128)(2,1)S(1)}, u32[]{:S(2)}) copy-start(bf16[24,1152]{1,0:T(8,128)(2,1)S(1)} %multiply_convert_fusion.2) | copy-start | bytes 165892
  72.4 5.2 %copy-start.3 = (f32[168,1024]{1,0:T(8,128)S(1)}, f32[168,1024]{1,0:T(8,128)}, u32[]{:S(2)}) copy-start(f32[168,1024]{1,0:T(8,128)} %get-tuple-element.21) | copy-start | bytes 2064388
  72.4 5.8 %copy-start.16 = (bf16[2048,1024]{1,0:T(8,128)(2,1)S(1)}, bf16[2048,1024]{1,0:T(8,128)(2,1)}, u32[]{:S(2)}) copy-start(bf16[2048,1024]{1,0:T(8,128)(2,1)} %param.19) | copy-start | bytes 12582916
  76.9 2.9 %copy-start.10 = (bf16[24,2048]{1,0:T(8,128)(2,1)}, bf16[24,2048]{1,0:T(8,128)(2,1)S(1)}, u32[]{:S(2)}) copy-start(bf16[24,2048]{1,0:T(8,128)(2,1)S(1)} %convolution_convert_fusion) | copy-start | bytes 294916
  77.5 0.6 copy-start.8
  79.7 38.7 %copy-start.5 = (f32[24,1152]{1,0:T(8,128)S(1)}, f32[24,1152]{1,0:T(8,128)}, u32[]{:S(2)}) copy-start(f32[24,1152]{1,0:T(8,128)} %copy-done.4) | copy-start | bytes 331780
  79.8 38.7 %copy-start.14 = (bf16[2,1152]{1,0:T(2,128)(2,1)S(1)}, bf16[2,1152]{1,0:T(2,128)(2,1)}, u32[]{:S(2)}) copy-start(bf16[2,1152]{1,0:T(2,128)(2,1)} %param.14) | copy-start | bytes 13828
  79.8 39.0 %copy-start.7 = (bf16[24,1152]{1,0:T(8,128)(2,1)S(1)}, bf16[24,1152]{1,0:T(8,128)(2,1)}, u32[]{:S(2)}) copy-start(bf16[24,1152]{1,0:T(8,128)(2,1)} %copy-done.6) | copy-start | bytes 165892
  79.8 40.7 %copy-start.12 = (bf16[24,1024]{1,0:T(8,128)(2,1)S(1)}, bf16[24,1024]{1,0:T(8,128)(2,1)}, u32[]{:S(2)}) copy-start(bf16[24,1024]{1,0:T(8,128)(2,1)} %convert_element_type.75) | copy-start | bytes 147460
  79.8 48.9 %copy-start.9 = (f32[24,1024]{1,0:T(8,128)S(1)}, f32[24,1024]{1,0:T(8,128)}, u32[]{:S(2)}) copy-start(f32[24,1024]{1,0:T(8,128)} %copy-done.8) | copy-start | bytes 294916
Sparse Core Ops, SparseCore 0:
  65.4 63.2 all-gather.1
